TPU v7x, 32 devices: a whole 2x2x4 slice. The times are simulated.
32 devices in a mesh: dp: 2 (over core), seq: 4 (over z), head: 4 (over y, x).
Axes of the slice: x: 2, y: 2, z: 4, core: 2. Of those that a mesh axis runs over, the one named last changes fastest.
Arguments:
- x_in: bfloat16 [2, 2048, 8192], P('dp', 'seq', 'head'), may hold values from -6 to 6
- b_in: bfloat16 [2, 2048, 128], P('dp', 'seq'), may hold values from -0.06591797 to 0.06591797
- c_in: bfloat16 [2, 2048, 128], P('dp', 'seq'), may hold values from -6 to 6
- rates: float32 [2, 128, 2048], P('dp', 'head', 'seq'), may hold values from 0 to 1, as said below
- skip: float32 [128], P('head'), may hold values from 0.1 to 1.9
- doc_lengths: int32 [2, 8], P('dp'), may hold values from 1 to 1536, 2048 in all within a row
- grad_y: bfloat16 [2, 2048, 8192], P('dp', ('seq', 'head')), may hold values from -6 to 6
Outputs:
- y_out: bfloat16 [2, 2048, 8192], P('dp', 'seq', 'head')
- grad_x: bfloat16 [2, 2048, 8192], P('dp', 'seq', 'head')
- grad_skip: float32 [128], P('head')
Inputs may be any that keep to these rules, and one draw needn't show every extreme that they name: rates are positive. `doc_lengths`: each row sums to 2048, and its largest entry is exactly 1536.
All inputs are finite; a program needn't handle non-finite values.
Results may differ from a plain program's by a relative error of at most 0.0024.
Values may be sent and summed in bfloat16 or wider, within the bound.
A program may use at most 128 MiB of HBM per device.

v0:
```python
import math

import jax
import jax.numpy as jnp
from jax import lax
from jax.sharding import PartitionSpec as P

HEAD_DIM = 64
GROUP = 128


def prefix(value, axis, combine, identity, reverse):
    count, index = (lax.axis_size(axis), lax.axis_index(axis))
    everything = jax.tree.map(lambda part: lax.all_gather(part, axis), value)
    start = jax.tree.map(
        lambda part, zero: jnp.broadcast_to(jnp.asarray(zero, part.dtype), part.shape),
        value,
        identity,
    )

    def turn(k, before):
        at = count - 1 - k if reverse else k
        reached = at > index if reverse else at < index
        new = combine(before, jax.tree.map(lambda part: part[at], everything))
        return jax.tree.map(lambda a, b: jnp.where(reached, a, b), new, before)

    return lax.fori_loop(0, count, turn, start)


def block_terms(b_rows, c_rows, rate_rows, doc_rows, prev_doc):
    running = jnp.cumsum(rate_rows, axis=1)
    inner = jnp.dot(c_rows, b_rows.T, preferred_element_type=jnp.float32)
    order = jnp.arange(doc_rows.shape[0], dtype=jnp.int32)
    same_doc = (doc_rows[:, None] == doc_rows[None, :]) & (order[:, None] >= order[None, :])
    gaps = running[:, :, None] - running[:, None, :]
    weights = jnp.exp(-jnp.where(same_doc[None], gaps, 1e30))
    scores = (weights * inner[None]).astype(jnp.bfloat16)
    to_end = jnp.where((doc_rows == doc_rows[-1])[None], jnp.exp(-(running[:, -1:] - running)), 0.0)
    from_prev = jnp.where((doc_rows == prev_doc)[None], jnp.exp(-running), 0.0)
    return (scores, to_end, from_prev)


def forward_block(carried_state, inputs_block):
    x_rows, b_rows, c_rows, scores, to_end, from_prev, end_prev = inputs_block
    inside = jnp.einsum("hts,shp->thp", scores, x_rows, preferred_element_type=jnp.float32)
    carried = from_prev.T[:, :, None] * jnp.einsum(
        "tn,hnp->thp", c_rows.astype(jnp.float32), carried_state, precision=lax.Precision.HIGHEST
    )
    weighted = to_end[:, :, None] * b_rows.astype(jnp.float32)[None]
    updated = end_prev[:, None, None] * carried_state + jnp.einsum(
        "hsn,shp->hnp", weighted, x_rows.astype(jnp.float32), precision=lax.Precision.HIGHEST
    )
    return (updated, inside + carried)


def backward_block(adjoint, inputs_block):
    g_rows, b_rows, c_rows, scores, to_end, from_prev, end_prev = inputs_block
    inside = jnp.einsum("hts,thp->shp", scores, g_rows, preferred_element_type=jnp.float32)
    carried = to_end.T[:, :, None] * jnp.einsum(
        "sn,hnp->shp", b_rows.astype(jnp.float32), adjoint, precision=lax.Precision.HIGHEST
    )
    weighted = from_prev[:, :, None] * c_rows.astype(jnp.float32)[None]
    updated = end_prev[:, None, None] * adjoint + jnp.einsum(
        "htn,thp->hnp", weighted, g_rows.astype(jnp.float32), precision=lax.Precision.HIGHEST
    )
    return (updated, inside + carried)


def local_sweeps(x_heads, grad_heads, b_rows, c_rows, rate_rows, doc_rows, prev_doc):
    row_count, heads_local, head_dim = x_heads.shape
    block_count = row_count // GROUP
    state_dim = b_rows.shape[1]
    blocks_x = x_heads.reshape(block_count, GROUP, heads_local, head_dim)
    blocks_g = grad_heads.reshape(block_count, GROUP, heads_local, head_dim)
    blocks_b = b_rows.reshape(block_count, GROUP, state_dim)
    blocks_c = c_rows.reshape(block_count, GROUP, state_dim)
    blocks_rate = rate_rows.reshape(heads_local, block_count, GROUP).transpose(1, 0, 2)
    blocks_doc = doc_rows.reshape(block_count, GROUP)
    prev_docs = jnp.concatenate([prev_doc[None], blocks_doc[:-1, -1]])
    scores, to_end, from_prev = jax.vmap(block_terms)(
        blocks_b, blocks_c, blocks_rate, blocks_doc, prev_docs
    )
    end_prev = from_prev[:, :, -1]
    zero_state = jnp.zeros((heads_local, state_dim, head_dim), jnp.float32)
    states_end, forward_out = lax.scan(
        forward_block,
        zero_state,
        (blocks_x, blocks_b, blocks_c, scores, to_end, from_prev, end_prev),
    )
    final_adjoint, backward_out = lax.scan(
        backward_block,
        zero_state,
        (blocks_g, blocks_b, blocks_c, scores, to_end, from_prev, end_prev),
        reverse=True,
    )
    shape_out = (row_count, heads_local, head_dim)
    return (
        forward_out.reshape(shape_out),
        states_end,
        backward_out.reshape(shape_out),
        final_adjoint,
    )


def combine(earlier, later):
    return (earlier[0] * later[0], later[0][..., None, None] * earlier[1] + later[1])


def shards(x_in, b_in, c_in, rates, skip, doc_lengths, grad_y):
    grad_local = lax.all_to_all(grad_y, "head", split_axis=2, concat_axis=1, tiled=True)
    seq_count, row_count, feature_count = x_in.shape
    heads_local = skip.shape[0]
    first_row = lax.axis_index("seq") * row_count
    token_positions = first_row - 1 + jnp.arange(row_count + 1, dtype=jnp.int32)
    doc_ends = jnp.cumsum(doc_lengths, axis=1)[:, :-1]
    docs_all = jnp.sum(
        (token_positions[None, :, None] >= doc_ends[:, None, :]).astype(jnp.int32), axis=2
    )
    documents = docs_all[:, 1:]
    prev_doc = docs_all[:, 0]
    x_heads = x_in.reshape(seq_count, row_count, heads_local, HEAD_DIM)
    grad_heads = grad_local.reshape(seq_count, row_count, heads_local, HEAD_DIM)
    forward_out, states_end, backward_out, final_adjoint = jax.vmap(local_sweeps)(
        x_heads, grad_heads, b_in, c_in, rates, documents, prev_doc
    )
    running = jnp.cumsum(rates, axis=2)
    unbroken = documents[:, -1] == prev_doc
    device_decay = jnp.where(unbroken[:, None], jnp.exp(-running[:, :, -1]), 0.0)
    identity_pair = (jnp.ones_like(device_decay), jnp.zeros_like(states_end))
    unused_decay, states_in = prefix(
        (device_decay, states_end), "seq", combine, identity_pair, False
    )
    other_decay, adjoint_in = prefix(
        (device_decay, final_adjoint), "seq", combine, identity_pair, True
    )
    weight_in = jnp.where(documents[:, None, :] == prev_doc[:, None, None], jnp.exp(-running), 0.0)
    weight_out = jnp.where(
        documents[:, None, :] == documents[:, None, -1:],
        jnp.exp(-(running[:, :, -1:] - running)),
        0.0,
    )
    entering = (
        jnp.einsum(
            "btn,bhnp->bthp", c_in.astype(jnp.float32), states_in, precision=lax.Precision.HIGHEST
        )
        * weight_in.transpose(0, 2, 1)[..., None]
    )
    leaving = (
        jnp.einsum(
            "bsn,bhnp->bshp", b_in.astype(jnp.float32), adjoint_in, precision=lax.Precision.HIGHEST
        )
        * weight_out.transpose(0, 2, 1)[..., None]
    )
    skip_gain = skip[None, None, :, None]
    out_values = (
        (forward_out + entering + skip_gain * x_heads.astype(jnp.float32))
        .astype(jnp.bfloat16)
        .reshape(seq_count, row_count, feature_count)
    )
    grad_values = (
        (backward_out + leaving + skip_gain * grad_heads.astype(jnp.float32))
        .astype(jnp.bfloat16)
        .reshape(seq_count, row_count, feature_count)
    )
    partial_value = jnp.einsum(
        "bthp,bthp->h", x_heads, grad_heads, preferred_element_type=jnp.float32
    )
    skip_sums = lax.psum(partial_value, ("dp", "seq"))
    tokens_all = lax.axis_size("dp") * seq_count * lax.axis_size("seq") * row_count * HEAD_DIM
    grad_skip = skip_sums / math.sqrt(tokens_all)
    return (out_values, grad_values, grad_skip)


def solution(mesh):
    placed = (
        P("dp", "seq", "head"),
        P("dp", "seq", None),
        P("dp", "seq", None),
        P("dp", "head", "seq"),
        P("head"),
        P("dp", None),
        P("dp", ("seq", "head"), None),
    )
    return jax.shard_map(
        shards,
        mesh=mesh,
        in_specs=placed,
        out_specs=(P("dp", "seq", "head"), P("dp", "seq", "head"), P("head")),
        check_vma=False,
    )
```

profile of v0, /device:TPU:0, one launch (start us, length us, event | category | flops | bytes accessed | tf_op | source)
XLA Modules:
  0.0 504.9 jit_solution(9707075332226923431)
XLA Ops:
  7.2 9.5 %copy.201 = bf16[1,128,8192]{1,0,2:T(2,128)(2,1)} copy(bf16[1,128,8192]{2,1,0:T(8,128)(2,1)} %param.21) | data formatting | bytes 4194304 | tf_op args[6]
  17.2 46.5 %reduce.13 = bf16[8192,128]{1,0:T(8,128)(2,1)} reduce(bf16[8192,1,128]{2,1,0:T(2,128)(2,1)} %bitcast.310, bf16[]{:T(256)} %broadcast.415), dimensions={1}, to_apply=%bitcast.227.reduce_sub_computation | reduce | bytes 4194306
  67.7 5.3 %all-to-all-start = ((bf16[4,2,131072]{2,1,0:T(2,128)(2,1)}), bf16[4,2,131072]{2,1,0:T(2,128)(2,1)}, u32[]{:S(2)}, u32[]{:S(2)}) async-start(bf16[4,2,131072]{2,1,0:T(2,128)(2,1)} %reshape.738), calls=%async_computation | async-start | bytes 4194304 | tf_op jit(solution)/shard_map/all_to_all | solution.py:110
  75.9 7.1 %reshape.732 = bf16[4,1,128,32,64]{4,3,2,0,1:T(8,128)(2,1)} reshape(bf16[1,512,2048]{2,1,0:T(8,128)(2,1)} %param.15) | data formatting | bytes 4194304 | tf_op jit(solution)/shard_map/vmap()/transpose;vmap()/reshape;reshape | solution.py:85
  83.0 6.5 %copy.190 = bf16[4,1,128,32,64]{2,4,3,1,0:T(8,128)(2,1)} copy(bf16[4,1,128,32,64]{4,3,2,0,1:T(8,128)(2,1)} %reshape.732) | data formatting | bytes 4194304
  98.2 128.7 %while.60 = (s32[]{:T(128)}, f32[1,32,128,64]{2,3,1,0:T(8,128)S(1)}, f32[4,1,128,32,64]{2,0,4,3,1:T(4,128)}, f32[4,1,32]{2,1,0:T(1,128)S(1)}, f32[4,1,32,128]{3,...) while((s32[]{:T(128)}, ...), condition=%wide.region_4.5_spmd.clone, body=%wide.region_3.4_spmd.clone.sunk | while | flops 874266624 | bytes 21268412 | solution.py:85
  103.9 26.4 %dynamic_update_slice.17 = f32[4,1,128,32,64]{2,0,4,3,1:T(4,128)} dynamic-update-slice(f32[4,1,128,32,64]{2,0,4,3,1:T(4,128)} %get-tuple-element.1106, f32[1,1,128,32,64]{2,0,4,3,1:T(1,128)S(1)} %bitcast.304, s32[]{:T(128)S(6)} %copy.252, s32[]{:T(128)} %constant.146.clone.1..sunk, s32[]{:T(128)} %constant.146.clone.1..sunk, s32[]{:T(128)} %constant.146.clone.1..sunk, s32[]{:T(128)} %constant.146.clone.1..sunk) | dynamic-update-slice | bytes 2097156 | tf_op jit(solution)/shard_map/vmap()/while/body/jit(dynamic_update_index_in_dim)/dynamic_update_slice | solution.py:85
  136.1 26.4 %dynamic_update_slice.17 = f32[4,1,128,32,64]{2,0,4,3,1:T(4,128)} dynamic-update-slice(f32[4,1,128,32,64]{2,0,4,3,1:T(4,128)} %get-tuple-element.1106, f32[1,1,128,32,64]{2,0,4,3,1:T(1,128)S(1)} %bitcast.304, s32[]{:T(128)S(6)} %copy.252, s32[]{:T(128)} %constant.146.clone.1..sunk, s32[]{:T(128)} %constant.146.clone.1..sunk, s32[]{:T(128)} %constant.146.clone.1..sunk, s32[]{:T(128)} %constant.146.clone.1..sunk) | dynamic-update-slice | bytes 2097156 | tf_op jit(solution)/shard_map/vmap()/while/body/jit(dynamic_update_index_in_dim)/dynamic_update_slice | solution.py:85
  168.3 26.4 %dynamic_update_slice.17 = f32[4,1,128,32,64]{2,0,4,3,1:T(4,128)} dynamic-update-slice(f32[4,1,128,32,64]{2,0,4,3,1:T(4,128)} %get-tuple-element.1106, f32[1,1,128,32,64]{2,0,4,3,1:T(1,128)S(1)} %bitcast.304, s32[]{:T(128)S(6)} %copy.252, s32[]{:T(128)} %constant.146.clone.1..sunk, s32[]{:T(128)} %constant.146.clone.1..sunk, s32[]{:T(128)} %constant.146.clone.1..sunk, s32[]{:T(128)} %constant.146.clone.1..sunk) | dynamic-update-slice | bytes 2097156 | tf_op jit(solution)/shard_map/vmap()/while/body/jit(dynamic_update_index_in_dim)/dynamic_update_slice | solution.py:85
  200.5 26.4 %dynamic_update_slice.17 = f32[4,1,128,32,64]{2,0,4,3,1:T(4,128)} dynamic-update-slice(f32[4,1,128,32,64]{2,0,4,3,1:T(4,128)} %get-tuple-element.1106, f32[1,1,128,32,64]{2,0,4,3,1:T(1,128)S(1)} %bitcast.304, s32[]{:T(128)S(6)} %copy.252, s32[]{:T(128)} %constant.146.clone.1..sunk, s32[]{:T(128)} %constant.146.clone.1..sunk, s32[]{:T(128)} %constant.146.clone.1..sunk, s32[]{:T(128)} %constant.146.clone.1..sunk) | dynamic-update-slice | bytes 2097156 | tf_op jit(solution)/shard_map/vmap()/while/body/jit(dynamic_update_index_in_dim)/dynamic_update_slice | solution.py:85
  238.7 133.4 %while.62 = (s32[]{:T(128)}, f32[1,32,128,64]{2,3,1,0:T(8,128)}, f32[4,1,128,32,64]{2,0,4,3,1:T(4,128)}, f32[4,1,32]{2,1,0:T(1,128)S(1)}, f32[4,1,32,128]{3,2,1,...) while((s32[]{:T(128)}, f32[1,32,128,64]{2,3,1,0:T(8,128)}, ...), condition=%wide.region_10.11_spmd.clone, body=%wide.region_9.10_spmd.clone.sunk | while | flops 874266624 | bytes 12883947 | solution.py:90
  244.7 26.4 %dynamic_update_slice.18 = f32[4,1,128,32,64]{2,0,4,3,1:T(4,128)} dynamic-update-slice(f32[4,1,128,32,64]{2,0,4,3,1:T(4,128)} %get-tuple-element.1164, f32[1,1,128,32,64]{2,0,4,3,1:T(1,128)S(1)} %bitcast.305, s32[]{:T(128)S(6)} %sub.111, s32[]{:T(128)} %constant.146.clone.1..sunk.2, s32[]{:T(128)} %constant.146.clone.1..sunk.2, s32[]{:T(128)} %constant.146.clone.1..sunk.2, s32[]{:T(128)} %constant.146.clone.1..sunk.2) | dynamic-update-slice | bytes 2097156 | tf_op jit(solution)/shard_map/vmap()/while/body/jit(dynamic_update_index_in_dim)/dynamic_update_slice | solution.py:85
  278.4 26.4 %dynamic_update_slice.18 = f32[4,1,128,32,64]{2,0,4,3,1:T(4,128)} dynamic-update-slice(f32[4,1,128,32,64]{2,0,4,3,1:T(4,128)} %get-tuple-element.1164, f32[1,1,128,32,64]{2,0,4,3,1:T(1,128)S(1)} %bitcast.305, s32[]{:T(128)S(6)} %sub.111, s32[]{:T(128)} %constant.146.clone.1..sunk.2, s32[]{:T(128)} %constant.146.clone.1..sunk.2, s32[]{:T(128)} %constant.146.clone.1..sunk.2, s32[]{:T(128)} %constant.146.clone.1..sunk.2) | dynamic-update-slice | bytes 2097156 | tf_op jit(solution)/shard_map/vmap()/while/body/jit(dynamic_update_index_in_dim)/dynamic_update_slice | solution.py:85
  312.0 26.4 %dynamic_update_slice.18 = f32[4,1,128,32,64]{2,0,4,3,1:T(4,128)} dynamic-update-slice(f32[4,1,128,32,64]{2,0,4,3,1:T(4,128)} %get-tuple-element.1164, f32[1,1,128,32,64]{2,0,4,3,1:T(1,128)S(1)} %bitcast.305, s32[]{:T(128)S(6)} %sub.111, s32[]{:T(128)} %constant.146.clone.1..sunk.2, s32[]{:T(128)} %constant.146.clone.1..sunk.2, s32[]{:T(128)} %constant.146.clone.1..sunk.2, s32[]{:T(128)} %constant.146.clone.1..sunk.2) | dynamic-update-slice | bytes 2097156 | tf_op jit(solution)/shard_map/vmap()/while/body/jit(dynamic_update_index_in_dim)/dynamic_update_slice | solution.py:85
  345.7 26.4 %dynamic_update_slice.18 = f32[4,1,128,32,64]{2,0,4,3,1:T(4,128)} dynamic-update-slice(f32[4,1,128,32,64]{2,0,4,3,1:T(4,128)} %get-tuple-element.1164, f32[1,1,128,32,64]{2,0,4,3,1:T(1,128)S(1)} %bitcast.305, s32[]{:T(128)S(6)} %sub.111, s32[]{:T(128)} %constant.146.clone.1..sunk.2, s32[]{:T(128)} %constant.146.clone.1..sunk.2, s32[]{:T(128)} %constant.146.clone.1..sunk.2, s32[]{:T(128)} %constant.146.clone.1..sunk.2) | dynamic-update-slice | bytes 2097156 | tf_op jit(solution)/shard_map/vmap()/while/body/jit(dynamic_update_index_in_dim)/dynamic_update_slice | solution.py:85
  376.1 5.5 %transpose.84 = f32[512,32,64]{0,2,1:T(8,128)} reshape(f32[4,1,128,32,64]{2,0,4,3,1:T(4,128)} %get-tuple-element.481) | data formatting | bytes 8388608 | tf_op jit(solution)/shard_map/vmap()/reshape;vmap()/transpose | solution.py:98
  386.3 12.5 %all-gather = f32[4,32,1]{1,2,0:T(1,128)S(1)} all-gather(f32[1,32,1]{1,2,0:T(1,128)S(1)} %get-tuple-element.891), channel_id=2, replica_groups=mesh['dp'=2,'seq'=4,'head'=4] {'seq'}, dimensions={0}, use_global_device_ids=true | all-gather | bytes 640 | tf_op jit(solution)/shard_map/all_gather | solution.py:14
  398.8 5.5 %transpose.86 = f32[512,32,64]{0,2,1:T(8,128)} reshape(f32[4,1,128,32,64]{2,0,4,3,1:T(4,128)} %get-tuple-element.484) | data formatting | bytes 8388608 | tf_op jit(solution)/shard_map/vmap()/reshape;vmap()/transpose | solution.py:100
  404.2 10.7 %copy.211 = bf16[1,4,128,2048]{2,1,3,0:T(4,128)(2,1)} copy(bf16[1,4,128,2048]{2,3,1,0:T(8,128)(2,1)S(1)} %bitcast.307) | data formatting | bytes 4194304 | tf_op jit(solution)/shard_map/all_to_all | solution.py:110
  420.9 15.6 %psum.7 = f32[32]{0:T(128)S(1)} all-reduce(f32[32]{0:T(128)S(1)} %fusion.50), channel_id=1, replica_groups=mesh['dp'=2,'seq'=4,'head'=4] {'dp','seq'}, use_global_device_ids=true, to_apply=%region_13.14 | all-reduce | flops 32 | bytes 256 | tf_op jit(solution)/shard_map/psum | solution.py:168
  437.0 19.2 %while.61 = (s32[]{:T(128)}, f32[1,32,128,64]{3,2,1,0:T(8,128)}, s32[]{:T(128)}, f32[4,1,32]{2,1,0:T(1,128)S(1)}, f32[4,1,32,128,64]{3,4,2,0,1:T(8,128)}, /*index=5*/s32[]{:T(128)}, s32[]{:T(128)}) while((s32[]{:T(128)}, f32[1,32,128,64]{3,2,1,0:T(8,128)}, s32[]{:T(128)}, f32[4,1,32]{2,1,0:T(1,128)S(1)}, ...), condition=%wide.region_8.9_spmd.clone, body=%wide.region_7.8_spmd.clone.sunk | while | flops 1048580 | bytes 7340529 | solution.py:27
  456.1 7.6 %fusion.56 = bf16[512,32,64]{0,2,1:T(8,128)(2,1)S(1)} fusion(f32[512,32,64]{0,2,1:T(8,128)} %transpose.84, bf16[512,32,64]{0,2,1:T(8,128)(2,1)} %bitcast.309, f32[1,32,128,64]{3,2,1,0:T(8,128)} %get-tuple-element.483, f32[32]{0:T(128)S(1)} %copy-done.10, f32[512,32]{0,1:T(8,128)S(1)} %copy.199, bf16[1,512,128]{2,1,0:T(8,128)(2,1)S(1)} %bitcast.318), kind=kOutput, calls=%fused_computation.70 | convolution fusion | flops 1616904192 | bytes 9633920 | tf_op jit(solution)/shard_map/btn,bhnp->bthp/dot_general | solution.py:143
  466.1 19.2 %while.63 = (s32[]{:T(128)}, f32[1,32,128,64]{3,2,1,0:T(8,128)}, s32[]{:T(128)}, f32[4,1,32]{2,1,0:T(1,128)S(1)}, f32[4,1,32,128,64]{3,4,2,0,1:T(8,128)}, /*index=5*/s32[]{:T(128)}, s32[]{:T(128)}, s32[]{:T(128)}, s32[]{:T(128)}) while((s32[]{:T(128)}, f32[1,32,128,64]{3,2,1,0:T(8,128)}, s32[]{:T(128)}, ...), condition=%wide.region_12.13_spmd.clone, body=%wide.region_11.12_spmd.clone.sunk | while | flops 1048584 | bytes 7340591 | solution.py:27
  485.2 8.9 %fusion.53 = bf16[512,32,64]{0,2,1:T(8,128)(2,1)} fusion(f32[512,32,64]{0,2,1:T(8,128)} %transpose.86, bf16[512,32,64]{0,2,1:T(8,128)(2,1)} %copy-done.4, f32[1,32,128,64]{3,2,1,0:T(8,128)} %get-tuple-element.486, f32[512,32]{0,1:T(8,128)S(1)} %copy.210, f32[32]{0:T(128)S(1)} %copy-done.10, bf16[1,512,128]{2,1,0:T(8,128)(2,1)S(1)} %bitcast.321), kind=kOutput, calls=%fused_computation.66 | convolution fusion | flops 1616904192 | bytes 9633920 | tf_op jit(solution)/shard_map/bsn,bhnp->bshp/dot_general | solution.py:149
  (191 shorter events, 136.3 us)
Async XLA Ops:
  7.2 67.0 %copy-start = (f32[1,32,512]{2,1,0:T(8,128)S(1)}, f32[1,32,512]{2,1,0:T(8,128)}, u32[]{:S(2)}) copy-start(f32[1,32,512]{2,1,0:T(8,128)} %param.18) | copy-start | bytes 196612
  67.7 5.3 %copy-start.13 = (s32[1,8]{1,0:T(1,128)S(1)}, s32[1,8]{1,0:T(1,128)}, u32[]{:S(2)}) copy-start(s32[1,8]{1,0:T(1,128)} %param.20) | copy-start | bytes 100
  67.7 160.5 %all-to-all-start = ((bf16[4,2,131072]{2,1,0:T(2,128)(2,1)}), bf16[4,2,131072]{2,1,0:T(2,128)(2,1)}, u32[]{:S(2)}, u32[]{:S(2)}) async-start(bf16[4,2,131072]{2,1,0:T(2,128)(2,1)} %reshape.738), calls=%async_computation | async-start | bytes 4194304 | tf_op jit(solution)/shard_map/all_to_all | solution.py:110
  73.0 363.9 %all-gather.6.cloned.1.call-start = ((), (), s32[]{:S(2)}) async-start(), calls=%async_computation.1 | async-start | bytes 5242880 | tf_op jit(solution)/shard_map/all_gather | solution.py:14
  73.4 0.8 copy-start.8
  83.0 8.1 %copy-start.5 = (bf16[1,512,128]{2,1,0:T(8,128)(2,1)S(1)}, bf16[1,512,128]{2,1,0:T(8,128)(2,1)}, u32[]{:S(2)}) copy-start(bf16[1,512,128]{2,1,0:T(8,128)(2,1)} %param.17) | copy-start | bytes 393220
  83.0 8.1 %copy-start.6 = (bf16[1,512,128]{2,1,0:T(8,128)(2,1)S(1)}, bf16[1,512,128]{2,1,0:T(8,128)(2,1)}, u32[]{:S(2)}) copy-start(bf16[1,512,128]{2,1,0:T(8,128)(2,1)} %param.16) | copy-start | bytes 393220
  98.2 1.6 copy-start.3
  130.4 1.6 copy-start.3
  162.6 1.6 copy-start.3
  194.8 1.6 copy-start.3
  226.9 1.0 copy-start.2
  227.9 238.1 %all-gather.8.cloned.1.call-start = ((), (), s32[]{:S(2)}) async-start(), calls=%async_computation.2 | async-start | bytes 5242880 | tf_op jit(solution)/shard_map/all_gather | solution.py:14
  244.7 26.4 %copy-start.12 = (f32[4,1,32]{2,1,0:T(1,128)S(1)}, f32[4,1,32]{2,1,0:T(1,128)}, u32[]{:S(2)}) copy-start(f32[4,1,32]{2,1,0:T(1,128)} %copy-done.11) | copy-start | bytes 1540 | tf_op jit(solution)/shard_map/vmap()/while
  271.1 0.6 copy-start.11
  278.3 26.4 %copy-start.12 = (f32[4,1,32]{2,1,0:T(1,128)S(1)}, f32[4,1,32]{2,1,0:T(1,128)}, u32[]{:S(2)}) copy-start(f32[4,1,32]{2,1,0:T(1,128)} %copy-done.11) | copy-start | bytes 1540 | tf_op jit(solution)/shard_map/vmap()/while
  304.8 0.6 copy-start.11
  312.0 26.4 %copy-start.12 = (f32[4,1,32]{2,1,0:T(1,128)S(1)}, f32[4,1,32]{2,1,0:T(1,128)}, u32[]{:S(2)}) copy-start(f32[4,1,32]{2,1,0:T(1,128)} %copy-done.11) | copy-start | bytes 1540 | tf_op jit(solution)/shard_map/vmap()/while
  345.7 26.4 %copy-start.12 = (f32[4,1,32]{2,1,0:T(1,128)S(1)}, f32[4,1,32]{2,1,0:T(1,128)}, u32[]{:S(2)}) copy-start(f32[4,1,32]{2,1,0:T(1,128)} %copy-done.11) | copy-start | bytes 1540 | tf_op jit(solution)/shard_map/vmap()/while
  376.1 5.5 %copy-start.7 = (f32[1,32,4,128]{3,1,2,0:T(8,128)S(1)}, f32[1,32,4,128]{3,1,2,0:T(8,128)}, u32[]{:S(2)}) copy-start(f32[1,32,4,128]{3,1,2,0:T(8,128)} %get-tuple-element.892) | copy-start | bytes 196612
  376.1 8.3 %copy-start.9 = (s32[1,513]{1,0:T(1,128)S(1)}, s32[1,513]{1,0:T(1,128)}, u32[]{:S(2)}) copy-start(s32[1,513]{1,0:T(1,128)} %copy-done.8) | copy-start | bytes 6160
  417.7 3.2 copy-start.4
  437.0 19.2 %copy-start.10 = (f32[32]{0:T(128)S(1)}, f32[32]{0:T(128)}, u32[]{:S(2)}) copy-start(f32[32]{0:T(128)} %param.19) | copy-start | bytes 388
  494.1 3.9 copy-start.1
  (2 other events, 1.2 us)
Sparse Core Ops, SparseCore 0:
  228.1 83.1 all-gather.5
  372.2 83.6 all-gather.7
where the time goes:
time: 512 us; the launch traced here: 505 us
  local copies, waits for them, and re-layouts  317 us (62%)
  other arithmetic  86.7 us (17%)
  matrix products  51.8 us (10%)
  blocking collectives  28.1 us (5%)
  between operations  15.5 us (3%)
  starting transfers between devices  5.59 us (1%)
    dynamic_update_slice x8, local copies, waits for them, and re-layouts, local_sweeps(): lax.scan(forward_block, zero_state, (blocks_x, blocks_b, blocks_c, scores...  211 us
    unnamed x6, other arithmetic  46.6 us
    unnamed x33, local copies, waits for them, and re-layouts  39.6 us
    select_n x8, other arithmetic, turn(): return jax.tree.map(lambda a, b: jnp.where(reached, a, b), new, before)  22.8 us
    psum x1, blocking collectives, shards(): skip_sums = lax.psum(partial_value, ('dp', 'seq'))  15.6 us
    dynamic_slice x16, local copies, waits for them, and re-layouts, turn(): new = combine(before, jax.tree.map(lambda part: part[at], everything))  15.2 us
    all_gather x1, blocking collectives, prefix(): everything = jax.tree.map(lambda part: lax.all_gather(part, axis), value)  12.5 us
    all_to_all x1, local copies, waits for them, and re-layouts, shards(): lax.all_to_all(grad_y, 'head', split_axis=2, concat_axis=1, tiled=True)  10.7 us
  transfers between devices with their start and end apart: 3, of which 0 were waited for; matrix products, arithmetic and copies ran while one was open for 70% of the time, Pallas kernels for 0%

commit v1 on v0

v1 whole, which is shorter than its diff:
```python
import functools
import math

import jax
import jax.numpy as jnp
from jax import lax
from jax.experimental import pallas as pl
from jax.experimental.pallas import tpu as pltpu
from jax.sharding import PartitionSpec as P

HEAD_DIM = 64
GROUP = 128
LANES = 128
PAIR = LANES // HEAD_DIM
EXACT = lax.Precision.HIGHEST
F32 = jnp.float32
BF16 = jnp.bfloat16


def split(value, axis):
    high = value.astype(BF16)
    low = (value - high.astype(F32)).astype(BF16)
    return jnp.concatenate([high, low], axis=axis)


def dot(a, b):
    return jnp.dot(a, b, preferred_element_type=F32)


def tdot(a, b):
    return lax.dot_general(a, b, (((0,), (0,)), ((), ())), preferred_element_type=F32)


def ndot(a, b):
    return lax.dot_general(a, b, (((1,), (1,)), ((), ())), preferred_element_type=F32)


def iota(axis):
    return lax.broadcasted_iota(jnp.int32, (GROUP, GROUP), axis)


def doc_of(position, ends):
    return sum((position >= end).astype(jnp.int32) for end in ends)


def doc_ends(lengths_ref):
    ends = []
    total = jnp.int32(0)
    for k in range(lengths_ref.shape[1] - 1):
        total = total + lengths_ref[0, k]
        ends.append(total)
    return ends


def block_masks(ends, first):
    here = doc_of(first + iota(0), ends)
    prev = doc_of(jnp.full((GROUP, GROUP), first - 1, jnp.int32), ends)
    last = doc_of(jnp.full((GROUP, GROUP), first + GROUP - 1, jnp.int32), ends)
    return here, (here == prev).astype(F32), (here == last).astype(F32)


def running_columns(rates, lower):
    return lax.dot_general(
        lower, rates, (((1,), (1,)), ((), ())), precision=EXACT, preferred_element_type=F32
    )


def pair_columns(columns, pair):
    wide = [
        jnp.broadcast_to(columns[:, h : h + 1], (GROUP, GROUP))
        for h in range(pair * PAIR, pair * PAIR + PAIR)
    ]
    lane_head = iota(1) // HEAD_DIM
    joined = wide[0]
    for h in range(1, PAIR):
        joined = jnp.where(lane_head == h, wide[h], joined)
    return wide, joined


def states_kernel(pairs, lengths_ref, x_ref, g_ref, b_ref, c_ref, rates_ref,
                  state_ref, adjoint_ref, decay_ref, partial_ref,
                  from_mask, to_mask, b_t, c_t):
    rows = x_ref.shape[0]
    blocks = rows // GROUP

    @pl.when(pl.program_id(0) == 0)
    def _():
        ends = doc_ends(lengths_ref)
        start = lax.axis_index("seq") * rows
        for k in range(blocks):
            span = slice(k * GROUP, (k + 1) * GROUP)
            _, from_mask[k], to_mask[k] = block_masks(ends, start + k * GROUP)
            bt = b_ref[span].astype(F32).T.astype(BF16)
            ct = c_ref[span].astype(F32).T.astype(BF16)
            b_t[k] = jnp.concatenate([bt, bt], axis=1)
            c_t[k] = jnp.concatenate([ct, ct], axis=1)

    lower = (iota(1) <= iota(0)).astype(F32)
    columns = [
        running_columns(rates_ref[0, :, k * GROUP : (k + 1) * GROUP], lower) for k in range(blocks)
    ]
    for pair in range(pairs):
        lanes = slice(pair * LANES, (pair + 1) * LANES)
        state = jnp.zeros((b_ref.shape[1], LANES), F32)
        adjoint = jnp.zeros_like(state)
        decay = jnp.ones((1, LANES), F32)
        partial = jnp.zeros((GROUP, LANES), F32)
        leaving = []
        for k in range(blocks):
            span = slice(k * GROUP, (k + 1) * GROUP)
            _, run = pair_columns(columns[k], pair)
            come = jnp.exp(-run) * from_mask[k]
            go = jnp.exp(run - run[GROUP - 1 : GROUP]) * to_mask[k]
            end = come[GROUP - 1 : GROUP]
            x = x_ref[span, lanes].astype(F32)
            g = g_ref[span, lanes].astype(F32)
            partial = partial + x * g
            state = end * state + dot(b_t[k], split(go * x, 0))
            decay = decay * end
            leaving.append((end, dot(c_t[k], split(come * g, 0))))
        for end, add in reversed(leaving):
            adjoint = end * adjoint + add
        state_ref[pair] = state
        adjoint_ref[pair] = adjoint
        decay_ref[pair] = decay
        partial_ref[pair] = jnp.sum(partial, axis=0, keepdims=True)


def chain_kernel(state_ref, adjoint_ref, decay_ref, into_ref, back_ref,
                 state_out, adjoint_out, send_f, recv_f, send_b, recv_b):
    count = lax.axis_size("seq")
    me = lax.axis_index("seq")
    later = jnp.minimum(me + 1, count - 1)
    earlier = jnp.maximum(me - 1, 0)
    first, last = me == 0, me == count - 1
    mesh_id = pl.DeviceIdType.MESH
    barrier = pltpu.get_barrier_semaphore()

    @pl.when(jnp.logical_not(first))
    def _():
        pl.semaphore_signal(barrier, inc=1, device_id={"seq": earlier}, device_id_type=mesh_id)

    @pl.when(jnp.logical_not(last))
    def _():
        pl.semaphore_signal(barrier, inc=1, device_id={"seq": later}, device_id_type=mesh_id)

    pl.semaphore_wait(
        barrier, jnp.where(first, 0, 1).astype(jnp.int32) + jnp.where(last, 0, 1).astype(jnp.int32)
    )

    def forward(q):
        return pltpu.make_async_remote_copy(
            src_ref=state_out.at[q], dst_ref=into_ref.at[q], send_sem=send_f.at[q],
            recv_sem=recv_f.at[q], device_id={"seq": later}, device_id_type=mesh_id)

    def backward(q):
        return pltpu.make_async_remote_copy(
            src_ref=adjoint_out.at[q], dst_ref=back_ref.at[q], send_sem=send_b.at[q],
            recv_sem=recv_b.at[q], device_id={"seq": earlier}, device_id_type=mesh_id)

    @pl.loop(0, state_ref.shape[0])
    def _(q):
        @pl.when(first)
        def _():
            into_ref[q] = jnp.zeros_like(into_ref[q])
            state_out[q] = state_ref[q]
            forward(q).start()

        @pl.when(jnp.logical_not(first) & jnp.logical_not(last))
        def _():
            forward(q).wait_recv()
            state_out[q] = decay_ref[q] * into_ref[q] + state_ref[q]
            forward(q).start()

        @pl.when(last)
        def _():
            back_ref[q] = jnp.zeros_like(back_ref[q])
            adjoint_out[q] = adjoint_ref[q]
            backward(q).start()

        @pl.when(jnp.logical_not(first) & jnp.logical_not(last))
        def _():
            backward(q).wait_recv()
            adjoint_out[q] = decay_ref[q] * back_ref[q] + adjoint_ref[q]
            backward(q).start()

    @pl.loop(0, state_ref.shape[0])
    def _(q):
        @pl.when(last)
        def _():
            forward(q).wait_recv()

        @pl.when(first)
        def _():
            backward(q).wait_recv()

        @pl.when(jnp.logical_not(last))
        def _():
            forward(q).wait_send()

        @pl.when(jnp.logical_not(first))
        def _():
            backward(q).wait_send()


def final_kernel(pairs, lengths_ref, x_ref, g_ref, b_ref, c_ref, rates_ref, skip_ref,
                 into_ref, back_ref, y_ref, gx_ref,
                 from_mask, to_mask, b_t, c_t, inner_ref):
    rows = x_ref.shape[0]
    blocks = rows // GROUP

    @pl.when(pl.program_id(0) == 0)
    def _():
        ends = doc_ends(lengths_ref)
        start = lax.axis_index("seq") * rows
        for k in range(blocks):
            span = slice(k * GROUP, (k + 1) * GROUP)
            at = start + k * GROUP
            here, from_mask[k], to_mask[k] = block_masks(ends, at)
            bt = b_ref[span].astype(F32).T.astype(BF16)
            ct = c_ref[span].astype(F32).T.astype(BF16)
            b_t[k] = jnp.concatenate([bt, bt], axis=1)
            c_t[k] = jnp.concatenate([ct, ct], axis=1)
            inner = ndot(c_ref[span], b_ref[span])
            same = (here == doc_of(at + iota(1), ends)) & (iota(0) >= iota(1))
            inner_ref[k] = jnp.where(same, inner, 0.0)

    lower = (iota(1) <= iota(0)).astype(F32)
    upper = (iota(0) <= iota(1)).astype(F32)
    lane_head = iota(1) // HEAD_DIM
    columns, lines = [], []
    for k in range(blocks):
        rates = rates_ref[0, :, k * GROUP : (k + 1) * GROUP]
        columns.append(running_columns(rates, lower))
        lines.append(jnp.dot(rates, upper, precision=EXACT, preferred_element_type=F32))

    def stack(value):
        zero = jnp.zeros_like(value)
        return jnp.concatenate([jnp.where(lane_head == h, value, zero) for h in range(PAIR)], axis=0)

    for pair in range(pairs):
        lanes = slice(pair * LANES, (pair + 1) * LANES)
        gain = skip_ref[pair]
        state = into_ref[pair]
        later = []
        for k in range(blocks):
            span = slice(k * GROUP, (k + 1) * GROUP)
            wide, run = pair_columns(columns[k], pair)
            come = jnp.exp(-run) * from_mask[k]
            go = jnp.exp(run - run[GROUP - 1 : GROUP]) * to_mask[k]
            end = come[GROUP - 1 : GROUP]
            inner = inner_ref[k]
            scores = [
                (jnp.exp(jnp.minimum(lines[k][pair * PAIR + h : pair * PAIR + h + 1] - wide[h], 0.0))
                 * inner).astype(BF16)
                for h in range(PAIR)
            ]
            x = x_ref[span, lanes]
            g = g_ref[span, lanes]
            xf = x.astype(F32)
            gf = g.astype(F32)
            c = c_ref[span]
            carried = come * dot(jnp.concatenate([c, c], axis=1), split(state, 0))
            inside = dot(jnp.concatenate(scores, axis=1), stack(x))
            y_ref[span, lanes] = (inside + carried + gain * xf).astype(BF16)
            if k + 1 < blocks:
                state = end * state + dot(b_t[k], split(go * xf, 0))
            back = tdot(jnp.concatenate(scores, axis=0), stack(g)) + gain * gf
            add = dot(c_t[k], split(come * gf, 0)) if k else None
            later.append((span, end, go, back, add))
        adjoint = back_ref[pair]
        for span, end, go, back, add in reversed(later):
            b = b_ref[span]
            carried = go * dot(jnp.concatenate([b, b], axis=1), split(adjoint, 0))
            gx_ref[span, lanes] = (back + carried).astype(BF16)
            if add is not None:
                adjoint = end * adjoint + add


def total_over(value, axis):
    count = lax.axis_size(axis)
    step = 1
    while step < count:
        other = lax.ppermute(value, axis, [(i, i ^ step) for i in range(count)])
        value = value + other
        step *= 2
    return value


def shards(x_in, b_in, c_in, rates, skip, doc_lengths, grad_y):
    _, rows, width = x_in.shape
    heads = skip.shape[0]
    state_dim = b_in.shape[2]
    all_pairs = width // LANES
    pairs = math.gcd(all_pairs, 2)
    steps = all_pairs // pairs
    blocks = rows // GROUP
    chunk = pairs * LANES

    grad_local = lax.all_to_all(grad_y, "head", split_axis=2, concat_axis=1, tiled=True)
    x, g, b, c = x_in[0], grad_local[0], b_in[0], c_in[0]
    rates_steps = rates.reshape(steps, pairs * PAIR, rows)
    gains = jnp.repeat(skip, HEAD_DIM).reshape(all_pairs, 1, LANES)

    wide = pl.BlockSpec((rows, chunk), lambda i: (0, i))
    whole = pl.BlockSpec((rows, state_dim), lambda i: (0, 0))
    lengths_spec = pl.BlockSpec(memory_space=pltpu.SMEM)
    rate_spec = pl.BlockSpec((1, pairs * PAIR, rows), lambda i: (i, 0, 0))
    state_spec = pl.BlockSpec((pairs, state_dim, LANES), lambda i: (i, 0, 0))
    line_spec = pl.BlockSpec((pairs, 1, LANES), lambda i: (i, 0, 0))
    state_shape = jax.ShapeDtypeStruct((all_pairs, state_dim, LANES), F32)
    line_shape = jax.ShapeDtypeStruct((all_pairs, 1, LANES), F32)
    setup = [
        pltpu.VMEM((blocks, GROUP, GROUP), F32),
        pltpu.VMEM((blocks, GROUP, GROUP), F32),
        pltpu.VMEM((blocks, state_dim, 2 * GROUP), BF16),
        pltpu.VMEM((blocks, state_dim, 2 * GROUP), BF16),
    ]

    states, adjoints, decays, partials = pl.pallas_call(
        functools.partial(states_kernel, pairs),
        grid=(steps,),
        in_specs=[lengths_spec, wide, wide, whole, whole, rate_spec],
        out_specs=[state_spec, state_spec, line_spec, line_spec],
        out_shape=[state_shape, state_shape, line_shape, line_shape],
        scratch_shapes=setup,
        name="states",
    )(doc_lengths, x, g, b, c, rates_steps)

    vmem = pl.BlockSpec(memory_space=pltpu.VMEM)
    into, back = pl.pallas_call(
        chain_kernel,
        in_specs=[vmem] * 3,
        out_specs=[vmem] * 2,
        out_shape=[state_shape] * 2,
        scratch_shapes=[
            pltpu.VMEM(state_shape.shape, F32),
            pltpu.VMEM(state_shape.shape, F32),
        ] + [pltpu.SemaphoreType.DMA((all_pairs,))] * 4,
        compiler_params=pltpu.CompilerParams(collective_id=0, has_side_effects=True),
        name="chain",
    )(states, adjoints, decays)

    sums = jnp.sum(partials.reshape(heads, HEAD_DIM), axis=1)
    sums = total_over(total_over(sums, "dp"), "seq")

    y, gx = pl.pallas_call(
        functools.partial(final_kernel, pairs),
        grid=(steps,),
        in_specs=[lengths_spec, wide, wide, whole, whole, rate_spec, line_spec, state_spec, state_spec],
        out_specs=[wide, wide],
        out_shape=[jax.ShapeDtypeStruct((rows, width), BF16)] * 2,
        scratch_shapes=setup + [pltpu.VMEM((blocks, GROUP, GROUP), F32)],
        cost_estimate=pl.CostEstimate(
            flops=24 * rows * GROUP * width, bytes_accessed=12 * rows * width, transcendentals=0
        ),
        name="final",
    )(doc_lengths, x, g, b, c, rates_steps, gains, into, back)

    tokens_all = lax.axis_size("dp") * lax.axis_size("seq") * rows * HEAD_DIM
    return y[None], gx[None], sums / math.sqrt(tokens_all)


def solution(mesh):
    placed = (
        P("dp", "seq", "head"),
        P("dp", "seq", None),
        P("dp", "seq", None),
        P("dp", "head", "seq"),
        P("head"),
        P("dp", None),
        P("dp", ("seq", "head"), None),
    )
    return jax.shard_map(
        shards,
        mesh=mesh,
        in_specs=placed,
        out_specs=(P("dp", "seq", "head"), P("dp", "seq", "head"), P("head")),
        check_vma=False,
    )
```

time: 512 us -> 251 us (0.49); the launches traced: 505 us -> 250 us
  local copies, waits for them, and re-layouts: 317 us -> 22.6 us
  Pallas kernels: 0 us -> 148 us
  matrix products: 51.8 us -> 0 us
  other arithmetic: 86.7 us -> 47.2 us
  blocking collectives: 28.1 us -> 0 us
  waiting for transfers between devices: 0.04 us -> 24.5 us
  between operations: 15.5 us -> 0.7 us
    dynamic_update_slice x8 -> x0, local copies, waits for them, and re-layouts: 211 us -> none  [local_sweeps(): lax.scan(forward_block, zero_state, (blocks_x, blocks_b, blocks_c, scores...]
    pallas_call x0 -> x3, Pallas kernels: none -> 148 us  [the longest x1 119 us: shards(): pl.pallas_call(chain_kernel, in_specs=[vmem] * 3, out_specs=[vmem] * 2, o...]
    dot_general x19 -> x0, matrix products: 47 us -> none  [the longest x4 9.77 us: backward_block(): jnp.einsum('htn,thp->hnp', weighted, g_rows.astype(jnp.float32), precisio...]
    all_to_all x1, waiting for transfers between devices: 0.01 us -> 24.1 us  [shards(): lax.all_to_all(grad_y, 'head', split_axis=2, concat_axis=1, tiled=True)]
    select_n x8 -> x0, other arithmetic: 22.8 us -> none  [turn(): return jax.tree.map(lambda a, b: jnp.where(reached, a, b), new, before)]
    unnamed x33 -> x9, local copies, waits for them, and re-layouts: 39.6 us -> 17.9 us
    psum x1 -> x0, blocking collectives: 15.6 us -> none  [shards(): skip_sums = lax.psum(partial_value, ('dp', 'seq'))]
    dynamic_slice x16 -> x0, local copies, waits for them, and re-layouts: 15.2 us -> none  [turn(): new = combine(before, jax.tree.map(lambda part: part[at], everything))]
  transfers between devices with their start and end apart: 3 -> 4, of which waited for: 0 -> 2; matrix products, arithmetic and copies ran while one was open for 70% -> 1% of each run, Pallas kernels for 0% -> 55%
where the time goes in v1:
time: 251 us; the launch traced here: 250 us
  Pallas kernels  148 us (59%)
  other arithmetic  47.2 us (19%)
  waiting for transfers between devices  24.5 us (10%)
  local copies, waits for them, and re-layouts  22.6 us (9%)
  starting transfers between devices  7.18 us (3%)
    pallas_call x1, Pallas kernels, shards(): pl.pallas_call(chain_kernel, in_specs=[vmem] * 3, out_specs=[vmem] * 2, o...  119 us
    unnamed x1, other arithmetic  45.2 us
    all_to_all x1, waiting for transfers between devices, shards(): lax.all_to_all(grad_y, 'head', split_axis=2, concat_axis=1, tiled=True)  24.1 us
    pallas_call x1, Pallas kernels, shards(): pl.pallas_call(functools.partial(final_kernel, pairs), grid=(steps,), in_...  18.8 us
    unnamed x9, local copies, waits for them, and re-layouts  17.9 us
    pallas_call x1, Pallas kernels, shards(): pl.pallas_call(functools.partial(states_kernel, pairs), grid=(steps,), in...  10.8 us
    all_to_all x1, starting transfers between devices, shards(): lax.all_to_all(grad_y, 'head', split_axis=2, concat_axis=1, tiled=True)  5.32 us
  transfers between devices with their start and end apart: 4, of which 2 were waited for; matrix products, arithmetic and copies ran while one was open for 1% of the time, Pallas kernels for 55%

profile of v1, /device:TPU:0, one launch (start us, length us, event | category | flops | bytes accessed | tf_op | source)
XLA Modules:
  0.0 250.4 jit_solution(3544987151044964181)
XLA Ops:
  0.6 9.5 %copy.14 = bf16[1,128,8192]{1,0,2:T(2,128)(2,1)} copy(bf16[1,128,8192]{2,1,0:T(8,128)(2,1)} %param.13) | data formatting | bytes 4194304 | tf_op args[6]
  10.1 0.5 broadcast.9
  10.6 45.2 %reduce.4 = bf16[8192,128]{1,0:T(8,128)(2,1)S(1)} reduce(bf16[8192,1,128]{2,1,0:T(2,128)(2,1)} %bitcast.11, bf16[]{:T(256)} %broadcast.9), dimensions={1}, to_apply=%bitcast.9.reduce_sub_computation | reduce | bytes 4194306
  55.8 2.1 reshape.31
  57.9 5.3 %all-to-all-start = ((bf16[4,2,131072]{2,1,0:T(2,128)(2,1)}), bf16[4,2,131072]{2,1,0:T(2,128)(2,1)S(1)}, u32[]{:S(2)}, u32[]{:S(2)}) async-start(bf16[4,2,131072]{2,1,0:T(2,128)(2,1)} %reshape.31), calls=%async_computation | async-start | bytes 4194304 | tf_op jit(solution)/shard_map/all_to_all | solution.py:300
  63.2 0.7 reshape.20.rates_ref
  63.9 0.1 broadcast_in_dim.13
  63.9 24.1 %all-to-all-done = bf16[4,2,131072]{2,1,0:T(2,128)(2,1)S(1)} async-done(((bf16[4,2,131072]{2,1,0:T(2,128)(2,1)}), bf16[4,2,131072]{2,1,0:T(2,128)(2,1)S(1)}, u32[]{:S(2)}, u32[]{:S(2)}) %all-to-all-start) | async-done | bytes 2097184 | tf_op jit(solution)/shard_map/all_to_all | solution.py:300
  88.1 3.3 %reshape.32 = bf16[8192,1,128]{2,1,0:T(2,128)(2,1)} reshape(bf16[4,2,131072]{2,1,0:T(2,128)(2,1)S(1)} %all-to-all-done) | data formatting | bytes 4194304
  91.4 2.5 copy.16
  93.9 2.7 %copy.15 = bf16[1,4,128,2048]{3,2,1,0:T(8,128)(2,1)} copy(bf16[1,4,128,2048]{2,3,1,0:T(8,128)(2,1)S(1)} %bitcast.13) | data formatting | bytes 4194304 | tf_op jit(solution)/shard_map/all_to_all | solution.py:300
  96.6 10.8 %states.1 = (f32[16,128,128]{2,1,0:T(8,128)}, f32[16,128,128]{2,1,0:T(8,128)}, f32[16,1,128]{2,1,0:T(1,128)}, f32[16,1,128]{2,1,0:T(1,128)}) custom-call(s32[1,8]{1,0:T(1,128)} %lengths_ref.3, bf16[512,2048]{1,0:T(8,128)(2,1)} %bitcast.16, bf16[512,2048]{1,0:T(8,128)(2,1)} %bitcast.14, bf16[512,128]{1,0:T(8,128)(2,1)} %bitcast.18, ...), custom_call_target="tpu_custom_call" | custom-call | tf_op jit(solution)/shard_map/states/pallas_call | solution.py:320
  107.4 0.5 broadcast.8
  107.9 1.4 reduce.3
  109.3 0.1 reshape.21
  109.4 0.1 reduce_sum.9
  109.6 0.1 broadcast_in_dim.14
  109.6 0.7 broadcast_in_dim.15.skip_ref
  110.3 0.4 collective-permute-done
  110.7 1.7 collective-permute-start.1
  112.4 118.6 %chain.1 = (f32[16,128,128]{2,1,0:T(8,128)}, f32[16,128,128]{2,1,0:T(8,128)}) custom-call(f32[16,128,128]{2,1,0:T(8,128)} %get-tuple-element.11.state_ref, f32[16,128,128]{2,1,0:T(8,128)} %get-tuple-element.12.adjoint_ref, f32[16,1,128]{2,1,0:T(1,128)} %get-tuple-element.13.decay_ref), custom_call_target="tpu_custom_call" | custom-call | tf_op jit(solution)/shard_map/chain/pallas_call | solution.py:331
  231.0 0.1 collective-permute-start.2
  231.1 18.8 %final.1 = (bf16[512,2048]{1,0:T(8,128)(2,1)}, bf16[512,2048]{1,0:T(8,128)(2,1)}) custom-call(s32[1,8]{1,0:T(1,128)} %lengths_ref.3, bf16[512,2048]{1,0:T(8,128)(2,1)} %bitcast.17, bf16[512,2048]{1,0:T(8,128)(2,1)} %bitcast.15, bf16[512,128]{1,0:T(8,128)(2,1)} %bitcast.19, bf16[512,128]{1,0:T(8,128)(2,1)} %bitcast.21, f32[8,4,512]{2,1,0:T(4,128)} %reshape.20.rates_ref, ...), custom_call_target="tpu_custom_call" | custom-call | flops 3221225472 | bytes 12582912 | tf_op jit(solution)/shard_map/final/pallas_call | solution.py:347
  249.9 0.5 add_multiply_fusion
  (9 shorter events, 0.1 us)
Async XLA Ops:
  57.9 5.3 %copy-start = (f32[1,32,512]{2,1,0:T(8,128)S(1)}, f32[1,32,512]{2,1,0:T(8,128)}, u32[]{:S(2)}) copy-start(f32[1,32,512]{2,1,0:T(8,128)} %param.10) | copy-start | bytes 196612
  57.9 6.0 %copy-start.1 = (f32[32]{0:T(128)S(1)}, f32[32]{0:T(128)}, u32[]{:S(2)}) copy-start(f32[32]{0:T(128)} %param.11) | copy-start | bytes 388
  57.9 30.2 %all-to-all-start = ((bf16[4,2,131072]{2,1,0:T(2,128)(2,1)}), bf16[4,2,131072]{2,1,0:T(2,128)(2,1)S(1)}, u32[]{:S(2)}, u32[]{:S(2)}) async-start(bf16[4,2,131072]{2,1,0:T(2,128)(2,1)} %reshape.31), calls=%async_computation | async-start | bytes 4194304 | tf_op jit(solution)/shard_map/all_to_all | solution.py:300
  109.5 1.2 collective-permute-start
  110.7 120.3 %collective-permute-start.1 = (f32[32]{0:T(128)S(1)}, f32[32]{0:T(128)S(1)}, u32[]{:S(2)}, u32[]{:S(2)}) collective-permute-start(f32[32]{0:T(128)S(1)} %add.9), channel_id=1, source_target_pairs={{0,4},{4,0},{8,12},{12,8},{1,5},{5,1},{9,13},{13,9},{2,6},{6,2},{1... | collective-permute-start | bytes 392 | tf_op jit(solution)/shard_map/ppermute | solution.py:284
  231.0 18.9 %collective-permute-start.2 = (f32[32]{0:T(128)S(1)}, f32[32]{0:T(128)S(1)}, u32[]{:S(2)}, u32[]{:S(2)}) collective-permute-start(f32[32]{0:T(128)S(1)} %add.10), channel_id=1, source_target_pairs={{0,8},{4,12},{8,0},{12,4},{1,9},{5,13},{9,1},{13,5},{2,10},{6,14},... | collective-permute-start | bytes 392 | tf_op jit(solution)/shard_map/ppermute | solution.py:284

commit v2 on v1

--- a/solution.py
+++ b/solution.py
@@ -77,63 +77,30 @@
     return wide, joined
 
 
-def states_kernel(pairs, lengths_ref, x_ref, g_ref, b_ref, c_ref, rates_ref,
-                  state_ref, adjoint_ref, decay_ref, partial_ref,
-                  from_mask, to_mask, b_t, c_t):
-    rows = x_ref.shape[0]
+LAG = 2
+
+
+def exchange_kernel(lengths_ref, x_ref, gy_ref, b_ref, c_ref, rates_ref,
+                    g_ref, into_ref, back_ref, partial_ref,
+                    state_out, adjoint_out, from_mask, to_mask, b_t, c_t,
+                    send_f, recv_f, send_b, recv_b, send_g, recv_g, own_sem):
+    rows, width = x_ref.shape
     blocks = rows // GROUP
-
-    @pl.when(pl.program_id(0) == 0)
-    def _():
-        ends = doc_ends(lengths_ref)
-        start = lax.axis_index("seq") * rows
-        for k in range(blocks):
-            span = slice(k * GROUP, (k + 1) * GROUP)
-            _, from_mask[k], to_mask[k] = block_masks(ends, start + k * GROUP)
-            bt = b_ref[span].astype(F32).T.astype(BF16)
-            ct = c_ref[span].astype(F32).T.astype(BF16)
-            b_t[k] = jnp.concatenate([bt, bt], axis=1)
-            c_t[k] = jnp.concatenate([ct, ct], axis=1)
-
-    lower = (iota(1) <= iota(0)).astype(F32)
-    columns = [
-        running_columns(rates_ref[0, :, k * GROUP : (k + 1) * GROUP], lower) for k in range(blocks)
-    ]
-    for pair in range(pairs):
-        lanes = slice(pair * LANES, (pair + 1) * LANES)
-        state = jnp.zeros((b_ref.shape[1], LANES), F32)
-        adjoint = jnp.zeros_like(state)
-        decay = jnp.ones((1, LANES), F32)
-        partial = jnp.zeros((GROUP, LANES), F32)
-        leaving = []
-        for k in range(blocks):
-            span = slice(k * GROUP, (k + 1) * GROUP)
-            _, run = pair_columns(columns[k], pair)
-            come = jnp.exp(-run) * from_mask[k]
-            go = jnp.exp(run - run[GROUP - 1 : GROUP]) * to_mask[k]
-            end = come[GROUP - 1 : GROUP]
-            x = x_ref[span, lanes].astype(F32)
-            g = g_ref[span, lanes].astype(F32)
-            partial = partial + x * g
-            state = end * state + dot(b_t[k], split(go * x, 0))
-            decay = decay * end
-            leaving.append((end, dot(c_t[k], split(come * g, 0))))
-        for end, add in reversed(leaving):
-            adjoint = end * adjoint + add
-        state_ref[pair] = state
-        adjoint_ref[pair] = adjoint
-        decay_ref[pair] = decay
-        partial_ref[pair] = jnp.sum(partial, axis=0, keepdims=True)
-
-
-def chain_kernel(state_ref, adjoint_ref, decay_ref, into_ref, back_ref,
-                 state_out, adjoint_out, send_f, recv_f, send_b, recv_b):
-    count = lax.axis_size("seq")
-    me = lax.axis_index("seq")
+    pair_count = width // LANES
+    own_rows = gy_ref.shape[0]
+    count, me = lax.axis_size("seq"), lax.axis_index("seq")
+    head_count, head_me = lax.axis_size("head"), lax.axis_index("head")
     later = jnp.minimum(me + 1, count - 1)
     earlier = jnp.maximum(me - 1, 0)
     first, last = me == 0, me == count - 1
     mesh_id = pl.DeviceIdType.MESH
+
+    own = pltpu.make_async_copy(
+        gy_ref.at[:, pl.ds(pl.multiple_of(head_me * width, LANES), width)],
+        g_ref.at[pl.ds(pl.multiple_of(head_me * own_rows, own_rows), own_rows)],
+        own_sem,
+    )
+    own.start()
     barrier = pltpu.get_barrier_semaphore()
 
     @pl.when(jnp.logical_not(first))
@@ -144,9 +111,26 @@
     def _():
         pl.semaphore_signal(barrier, inc=1, device_id={"seq": later}, device_id_type=mesh_id)
 
+    @pl.loop(1, head_count)
+    def _(i):
+        pl.semaphore_signal(
+            barrier, inc=1, device_id={"head": lax.rem(head_me + i, head_count)},
+            device_id_type=mesh_id)
+
     pl.semaphore_wait(
-        barrier, jnp.where(first, 0, 1).astype(jnp.int32) + jnp.where(last, 0, 1).astype(jnp.int32)
-    )
+        barrier, head_count - 1 + jnp.where(first, 0, 1).astype(jnp.int32)
+        + jnp.where(last, 0, 1).astype(jnp.int32))
+
+    def lanes_of(q):
+        return pl.ds(pl.multiple_of(q * LANES, LANES), LANES)
+
+    def cotangent(i, q):
+        peer = lax.rem(head_me + i, head_count)
+        return pltpu.make_async_remote_copy(
+            src_ref=gy_ref.at[:, pl.ds(pl.multiple_of(peer * width + q * LANES, LANES), LANES)],
+            dst_ref=g_ref.at[pl.ds(pl.multiple_of(head_me * own_rows, own_rows), own_rows), lanes_of(q)],
+            send_sem=send_g.at[i - 1, q], recv_sem=recv_g.at[i - 1, q],
+            device_id={"head": peer}, device_id_type=mesh_id)
 
     def forward(q):
         return pltpu.make_async_remote_copy(
@@ -158,41 +142,108 @@
             src_ref=adjoint_out.at[q], dst_ref=back_ref.at[q], send_sem=send_b.at[q],
             recv_sem=recv_b.at[q], device_id={"seq": earlier}, device_id_type=mesh_id)
 
-    @pl.loop(0, state_ref.shape[0])
+    @pl.loop(0, pair_count)
     def _(q):
+        @pl.loop(1, head_count)
+        def _(i):
+            cotangent(i, q).start()
+
+    ends = doc_ends(lengths_ref)
+    for k in range(blocks):
+        span = slice(k * GROUP, (k + 1) * GROUP)
+        _, from_mask[k], to_mask[k] = block_masks(ends, me * rows + k * GROUP)
+        bt = b_ref[span].astype(F32).T.astype(BF16)
+        ct = c_ref[span].astype(F32).T.astype(BF16)
+        b_t[k] = jnp.concatenate([bt, bt], axis=1)
+        c_t[k] = jnp.concatenate([ct, ct], axis=1)
+    own.wait()
+    lower = (iota(1) <= iota(0)).astype(F32)
+
+    def runs_of(q):
+        runs = []
+        for k in range(blocks):
+            columns = running_columns(rates_ref[q, :, k * GROUP : (k + 1) * GROUP], lower)
+            runs.append(pair_columns(columns, 0)[1])
+        return runs
+
+    def forward_step(q):
+        state = jnp.zeros((b_ref.shape[1], LANES), F32)
+        decay = jnp.ones((1, LANES), F32)
+        for k, run in enumerate(runs_of(q)):
+            total = run[GROUP - 1 : GROUP]
+            go = jnp.exp(run - total) * to_mask[k]
+            end = jnp.exp(-total) * from_mask[k, GROUP - 1 : GROUP]
+            x = x_ref[k * GROUP : (k + 1) * GROUP, lanes_of(q)].astype(F32)
+            state = end * state + dot(b_t[k], split(go * x, 0))
+            decay = decay * end
+
         @pl.when(first)
         def _():
-            into_ref[q] = jnp.zeros_like(into_ref[q])
-            state_out[q] = state_ref[q]
+            into_ref[q] = jnp.zeros_like(state)
+            state_out[q] = state
             forward(q).start()
 
-        @pl.when(jnp.logical_not(first) & jnp.logical_not(last))
+        @pl.when(jnp.logical_not(first))
         def _():
             forward(q).wait_recv()
-            state_out[q] = decay_ref[q] * into_ref[q] + state_ref[q]
-            forward(q).start()
+
+            @pl.when(jnp.logical_not(last))
+            def _():
+                state_out[q] = decay * into_ref[q] + state
+                forward(q).start()
+
+    def backward_step(q):
+        @pl.loop(1, head_count)
+        def _(i):
+            cotangent(i, q).wait_recv()
+
+        adjoint = jnp.zeros((b_ref.shape[1], LANES), F32)
+        decay = jnp.ones((1, LANES), F32)
+        partial = jnp.zeros((GROUP, LANES), F32)
+        runs = runs_of(q)
+        for k in reversed(range(blocks)):
+            come = jnp.exp(-runs[k]) * from_mask[k]
+            end = come[GROUP - 1 : GROUP]
+            x = x_ref[k * GROUP : (k + 1) * GROUP, lanes_of(q)].astype(F32)
+            g = g_ref[k * GROUP : (k + 1) * GROUP, lanes_of(q)].astype(F32)
+            partial = partial + x * g
+            adjoint = end * adjoint + dot(c_t[k], split(come * g, 0))
+            decay = decay * end
+        partial_ref[q] = jnp.sum(partial, axis=0, keepdims=True)
 
         @pl.when(last)
         def _():
-            back_ref[q] = jnp.zeros_like(back_ref[q])
-            adjoint_out[q] = adjoint_ref[q]
+            back_ref[q] = jnp.zeros_like(adjoint)
+            adjoint_out[q] = adjoint
             backward(q).start()
 
-        @pl.when(jnp.logical_not(first) & jnp.logical_not(last))
+        @pl.when(jnp.logical_not(last))
         def _():
             backward(q).wait_recv()
-            adjoint_out[q] = decay_ref[q] * back_ref[q] + adjoint_ref[q]
-            backward(q).start()
-
-    @pl.loop(0, state_ref.shape[0])
+
+            @pl.when(jnp.logical_not(first))
+            def _():
+                adjoint_out[q] = decay * back_ref[q] + adjoint
+                backward(q).start()
+
+    @pl.loop(0, pair_count + LAG * (count - 1))
+    def _(t):
+        q = t - LAG * me
+        r = t - LAG * (count - 1 - me)
+
+        @pl.when((q >= 0) & (q < pair_count))
+        def _():
+            forward_step(q)
+
+        @pl.when((r >= 0) & (r < pair_count))
+        def _():
+            backward_step(r)
+
+    @pl.loop(0, pair_count)
     def _(q):
-        @pl.when(last)
-        def _():
-            forward(q).wait_recv()
-
-        @pl.when(first)
-        def _():
-            backward(q).wait_recv()
+        @pl.loop(1, head_count)
+        def _(i):
+            cotangent(i, q).wait_send()
 
         @pl.when(jnp.logical_not(last))
         def _():
@@ -297,8 +348,7 @@
     blocks = rows // GROUP
     chunk = pairs * LANES
 
-    grad_local = lax.all_to_all(grad_y, "head", split_axis=2, concat_axis=1, tiled=True)
-    x, g, b, c = x_in[0], grad_local[0], b_in[0], c_in[0]
+    x, b, c = x_in[0], b_in[0], c_in[0]
     rates_steps = rates.reshape(steps, pairs * PAIR, rows)
     gains = jnp.repeat(skip, HEAD_DIM).reshape(all_pairs, 1, LANES)
 
@@ -317,29 +367,19 @@
         pltpu.VMEM((blocks, state_dim, 2 * GROUP), BF16),
     ]
 
-    states, adjoints, decays, partials = pl.pallas_call(
-        functools.partial(states_kernel, pairs),
-        grid=(steps,),
-        in_specs=[lengths_spec, wide, wide, whole, whole, rate_spec],
-        out_specs=[state_spec, state_spec, line_spec, line_spec],
-        out_shape=[state_shape, state_shape, line_shape, line_shape],
-        scratch_shapes=setup,
-        name="states",
-    )(doc_lengths, x, g, b, c, rates_steps)
-
     vmem = pl.BlockSpec(memory_space=pltpu.VMEM)
-    into, back = pl.pallas_call(
-        chain_kernel,
-        in_specs=[vmem] * 3,
-        out_specs=[vmem] * 2,
-        out_shape=[state_shape] * 2,
-        scratch_shapes=[
-            pltpu.VMEM(state_shape.shape, F32),
-            pltpu.VMEM(state_shape.shape, F32),
-        ] + [pltpu.SemaphoreType.DMA((all_pairs,))] * 4,
+    peers = lax.axis_size("head") - 1
+    dma = pltpu.SemaphoreType.DMA
+    g, into, back, partials = pl.pallas_call(
+        exchange_kernel,
+        in_specs=[lengths_spec] + [vmem] * 5,
+        out_specs=[vmem] * 4,
+        out_shape=[jax.ShapeDtypeStruct((rows, width), BF16), state_shape, state_shape, line_shape],
+        scratch_shapes=[pltpu.VMEM(state_shape.shape, F32)] * 2 + setup
+        + [dma((all_pairs,))] * 4 + [dma((peers, all_pairs))] * 2 + [dma],
         compiler_params=pltpu.CompilerParams(collective_id=0, has_side_effects=True),
-        name="chain",
-    )(states, adjoints, decays)
+        name="exchange",
+    )(doc_lengths, x, grad_y[0], b, c, rates.reshape(all_pairs, PAIR, rows))
 
     sums = jnp.sum(partials.reshape(heads, HEAD_DIM), axis=1)
     sums = total_over(total_over(sums, "dp"), "seq")

time: 251 us -> 80.1 us (0.32)
  Pallas kernels: 148 us -> 70.3 us
  other arithmetic: 47.2 us -> 2 us
  waiting for transfers between devices: 24.5 us -> 3.2 us
  local copies, waits for them, and re-layouts: 22.6 us -> 3.6 us
  starting transfers between devices: 7.18 us -> 0.07 us
    pallas_call x2 -> x1, Pallas kernels: 129 us -> 51.6 us  [shards(): pl.pallas_call(exchange_kernel, in_specs=[lengths_spec] + [vmem] * 5, out...]
    unnamed x1 -> x0, other arithmetic: 45.2 us -> none
    all_to_all x1 -> x0, waiting for transfers between devices: 24.1 us -> none  [shards(): lax.all_to_all(grad_y, 'head', split_axis=2, concat_axis=1, tiled=True)]
    unnamed x9 -> x4, local copies, waits for them, and re-layouts: 17.9 us -> 0.01 us
    all_to_all x1 -> x0, starting transfers between devices: 5.32 us -> none  [shards(): lax.all_to_all(grad_y, 'head', split_axis=2, concat_axis=1, tiled=True)]
    ppermute x3, waiting for transfers between devices: 0.38 us -> 3.2 us  [total_over(): other = lax.ppermute(value, axis, [(i, i ^ step) for i in range(count)])]
    all_to_all x1 -> x0, local copies, waits for them, and re-layouts: 2.7 us -> none  [shards(): lax.all_to_all(grad_y, 'head', split_axis=2, concat_axis=1, tiled=True)]
  transfers between devices with their start and end apart: 4 -> 3, of which waited for: 2 -> 2; matrix products, arithmetic and copies ran while one was open for 1% -> 2% of each run, Pallas kernels for 55% -> 23%
where the time goes in v2:
time: 80.1 us; the launch traced here: 79.9 us
  Pallas kernels  70.3 us (88%)
  local copies, waits for them, and re-layouts  3.6 us (4%)
  waiting for transfers between devices  3.2 us (4%)
  other arithmetic  2 us (2%)
    pallas_call x1, Pallas kernels, shards(): pl.pallas_call(exchange_kernel, in_specs=[lengths_spec] + [vmem] * 5, out...  51.6 us
    pallas_call x1, Pallas kernels, shards(): pl.pallas_call(functools.partial(final_kernel, pairs), grid=(steps,), in_...  18.8 us
    ppermute x3, waiting for transfers between devices, total_over(): other = lax.ppermute(value, axis, [(i, i ^ step) for i in range(count)])  3.2 us
  transfers between devices with their start and end apart: 3, of which 2 were waited for; matrix products, arithmetic and copies ran while one was open for 2% of the time, Pallas kernels for 23%

profile of v2, /device:TPU:0, one launch (start us, length us, event | category | flops | bytes accessed | tf_op | source)
XLA Modules:
  0.0 79.9 jit_solution(794830231158422953)
XLA Ops:
  0.6 1.5 %reshape.22.rates_ref = f32[16,2,512]{2,1,0:T(2,128)} reshape(f32[1,32,512]{2,1,0:T(8,128)} %param.10) | data formatting | bytes 131072 | tf_op jit(solution)/shard_map/reshape | solution.py:382
  2.1 0.0 copy-start
  2.1 0.0 copy-start.1
  2.1 51.6 %exchange.1 = (bf16[512,2048]{1,0:T(8,128)(2,1)}, f32[16,128,128]{2,1,0:T(8,128)}, f32[16,128,128]{2,1,0:T(8,128)}, f32[16,1,128]{2,1,0:T(1,128)}) custom-call(s32[1,8]{1,0:T(1,128)} %lengths_ref.3, bf16[512,2048]{1,0:T(8,128)(2,1)} %bitcast.7, bf16[128,8192]{1,0:T(8,128)(2,1)} %bitcast.6, bf16[512,128]{1,0:T(8,128)(2,1)} %bitcast.9, ...), custom_call_target="tpu_custom_call" | custom-call | tf_op jit(solution)/shard_map/exchange/pallas_call | solution.py:373
  53.7 0.5 broadcast.8
  54.2 1.4 %reduce.3 = f32[16,128]{1,0:T(8,128)S(1)} reduce(f32[16,1,128]{2,1,0:T(1,128)} %get-tuple-element.14, f32[]{:T(128)} %broadcast.8), dimensions={1}, to_apply=%get-tuple-element.14.reduce_sub_computation.3 | reduce | bytes 16388 | tf_op jit(solution)/shard_map/exchange/pallas_call | solution.py:373
  55.6 0.1 reshape.24
  55.7 0.1 reduce_sum.9
  55.8 0.1 collective-permute-start
  55.9 0.0 copy-done
  55.9 0.7 reshape.23.rates_ref
  56.5 0.0 copy-done.1
  56.5 0.1 broadcast_in_dim.13
  56.6 0.4 collective-permute-done
  57.0 0.0 collective-permute-start.1
  57.0 0.1 broadcast_in_dim.14
  57.1 0.7 broadcast_in_dim.15.skip_ref
  57.8 2.8 %collective-permute-done.1 = f32[32]{0:T(128)S(1)} collective-permute-done((f32[32]{0:T(128)S(1)}, f32[32]{0:T(128)S(1)}, u32[]{:S(2)}, u32[]{:S(2)}) %collective-permute-start.1) | collective-permute-done | bytes 160 | tf_op jit(solution)/shard_map/ppermute | solution.py:335
  60.6 0.0 collective-permute-start.2
  60.6 18.8 %final.1 = (bf16[512,2048]{1,0:T(8,128)(2,1)}, bf16[512,2048]{1,0:T(8,128)(2,1)}) custom-call(s32[1,8]{1,0:T(1,128)} %lengths_ref.3, bf16[512,2048]{1,0:T(8,128)(2,1)} %bitcast.8, bf16[512,2048]{1,0:T(8,128)(2,1)} %get-tuple-element.9.g_ref, bf16[512,128]{1,0:T(8,128)(2,1)} %bitcast.10, bf16[512,128]{1,0:T(8,128)(2,1)} %bitcast.12, ...), custom_call_target="tpu_custom_call" | custom-call | flops 3221225472 | bytes 12582912 | tf_op jit(solution)/shard_map/final/pallas_call | solution.py:387
  79.4 0.0 collective-permute-done.2
  79.4 0.5 add_multiply_fusion
  (2 shorter events, 0.0 us)
Async XLA Ops:
  2.1 53.7 %copy-start = (f32[1,32,512]{2,1,0:T(8,128)S(1)}, f32[1,32,512]{2,1,0:T(8,128)}, u32[]{:S(2)}) copy-start(f32[1,32,512]{2,1,0:T(8,128)} %param.10) | copy-start | bytes 196612
  2.1 54.4 %copy-start.1 = (f32[32]{0:T(128)S(1)}, f32[32]{0:T(128)}, u32[]{:S(2)}) copy-start(f32[32]{0:T(128)} %param.11) | copy-start | bytes 388
  55.8 1.2 %collective-permute-start = (f32[32]{0:T(128)S(1)}, f32[32]{0:T(128)S(1)}, u32[]{:S(2)}, u32[]{:S(2)}) collective-permute-start(f32[32]{0:T(128)S(1)} %reduce_sum.9), channel_id=1, source_target_pairs={{0,16},{16,0},{1,17},{17,1},{2,18},{18,2},{3,19},{19,3},{4,20},{20... | collective-permute-start | bytes 392 | tf_op jit(solution)/shard_map/ppermute | solution.py:335
  57.0 3.6 %collective-permute-start.1 = (f32[32]{0:T(128)S(1)}, f32[32]{0:T(128)S(1)}, u32[]{:S(2)}, u32[]{:S(2)}) collective-permute-start(f32[32]{0:T(128)S(1)} %add.9), channel_id=1, source_target_pairs={{0,4},{4,0},{8,12},{12,8},{1,5},{5,1},{9,13},{13,9},{2,6},{6,2},{1... | collective-permute-start | bytes 392 | tf_op jit(solution)/shard_map/ppermute | solution.py:335
  60.6 18.8 %collective-permute-start.2 = (f32[32]{0:T(128)S(1)}, f32[32]{0:T(128)S(1)}, u32[]{:S(2)}, u32[]{:S(2)}) collective-permute-start(f32[32]{0:T(128)S(1)} %add.10), channel_id=1, source_target_pairs={{0,8},{4,12},{8,0},{12,4},{1,9},{5,13},{9,1},{13,5},{2,10},{6,14},... | collective-permute-start | bytes 392 | tf_op jit(solution)/shard_map/ppermute | solution.py:335

commit v3 on v2

v3 whole, which is shorter than its diff:
```python
import functools
import math

import jax
import jax.numpy as jnp
from jax import lax
from jax.experimental import pallas as pl
from jax.experimental.pallas import tpu as pltpu
from jax.sharding import PartitionSpec as P

HEAD_DIM = 64
GROUP = 128
LANES = 128
PAIR = LANES // HEAD_DIM
EXACT = lax.Precision.HIGHEST
F32 = jnp.float32
BF16 = jnp.bfloat16


def split(value, axis):
    high = value.astype(BF16)
    low = (value - high.astype(F32)).astype(BF16)
    return jnp.concatenate([high, low], axis=axis)


def dot(a, b):
    return jnp.dot(a, b, preferred_element_type=F32)


def tdot(a, b):
    return lax.dot_general(a, b, (((0,), (0,)), ((), ())), preferred_element_type=F32)


def ndot(a, b):
    return lax.dot_general(a, b, (((1,), (1,)), ((), ())), preferred_element_type=F32)


def iota(axis):
    return lax.broadcasted_iota(jnp.int32, (GROUP, GROUP), axis)


def doc_of(position, ends):
    return sum((position >= end).astype(jnp.int32) for end in ends)


def doc_ends(lengths_ref):
    ends = []
    total = jnp.int32(0)
    for k in range(lengths_ref.shape[1] - 1):
        total = total + lengths_ref[0, k]
        ends.append(total)
    return ends


def block_masks(ends, first):
    here = doc_of(first + iota(0), ends)
    prev = doc_of(jnp.full((GROUP, GROUP), first - 1, jnp.int32), ends)
    last = doc_of(jnp.full((GROUP, GROUP), first + GROUP - 1, jnp.int32), ends)
    return here, (here == prev).astype(F32), (here == last).astype(F32)


def running_columns(rates, lower):
    return lax.dot_general(
        lower, rates, (((1,), (1,)), ((), ())), precision=EXACT, preferred_element_type=F32
    )


def pair_columns(columns, pair):
    wide = [
        jnp.broadcast_to(columns[:, h : h + 1], (GROUP, GROUP))
        for h in range(pair * PAIR, pair * PAIR + PAIR)
    ]
    lane_head = iota(1) // HEAD_DIM
    joined = wide[0]
    for h in range(1, PAIR):
        joined = jnp.where(lane_head == h, wide[h], joined)
    return wide, joined


LAG = 2


def exchange_kernel(scale, lengths_ref, x_ref, gy_ref, b_ref, c_ref, rates_ref, skip_ref,
                    y_ref, gx_ref, sums_ref,
                    g_ref, into_ref, back_ref, partial_ref, gathered_ref,
                    state_out, adjoint_out, from_mask, to_mask, b_t, c_t, inner_ref, inner_t_ref,
                    send_f, recv_f, send_b, recv_b, send_g, recv_g, send_p, recv_p, own_sem):
    rows, width = x_ref.shape
    blocks = rows // GROUP
    pair_count = width // LANES
    own_rows = gy_ref.shape[0]
    count, me = lax.axis_size("seq"), lax.axis_index("seq")
    head_count, head_me = lax.axis_size("head"), lax.axis_index("head")
    later = jnp.minimum(me + 1, count - 1)
    earlier = jnp.maximum(me - 1, 0)
    first, last = me == 0, me == count - 1
    mesh_id = pl.DeviceIdType.MESH

    own = pltpu.make_async_copy(
        gy_ref.at[:, pl.ds(pl.multiple_of(head_me * width, LANES), width)],
        g_ref.at[pl.ds(pl.multiple_of(head_me * own_rows, own_rows), own_rows)],
        own_sem,
    )
    own.start()
    barrier = pltpu.get_barrier_semaphore()

    copies = lax.axis_size("dp") * count
    copy_me = lax.axis_index("dp") * count + me

    def copy_peer(i):
        other = lax.rem(copy_me + i, copies)
        return {"dp": other // count, "seq": lax.rem(other, count)}

    @pl.loop(1, copies)
    def _(i):
        pl.semaphore_signal(barrier, inc=1, device_id=copy_peer(i), device_id_type=mesh_id)

    @pl.loop(1, head_count)
    def _(i):
        pl.semaphore_signal(
            barrier, inc=1, device_id={"head": lax.rem(head_me + i, head_count)},
            device_id_type=mesh_id)

    pl.semaphore_wait(barrier, head_count - 1 + copies - 1)

    def part(i):
        return pltpu.make_async_remote_copy(
            src_ref=partial_ref, dst_ref=gathered_ref.at[copy_me], send_sem=send_p.at[i - 1],
            recv_sem=recv_p.at[i - 1], device_id=copy_peer(i), device_id_type=mesh_id)

    def lanes_of(q):
        return pl.ds(pl.multiple_of(q * LANES, LANES), LANES)

    def cotangent(i, q):
        peer = lax.rem(head_me + i, head_count)
        return pltpu.make_async_remote_copy(
            src_ref=gy_ref.at[:, pl.ds(pl.multiple_of(peer * width + q * LANES, LANES), LANES)],
            dst_ref=g_ref.at[pl.ds(pl.multiple_of(head_me * own_rows, own_rows), own_rows), lanes_of(q)],
            send_sem=send_g.at[i - 1, q], recv_sem=recv_g.at[i - 1, q],
            device_id={"head": peer}, device_id_type=mesh_id)

    def forward(q):
        return pltpu.make_async_remote_copy(
            src_ref=state_out.at[q], dst_ref=into_ref.at[q], send_sem=send_f.at[q],
            recv_sem=recv_f.at[q], device_id={"seq": later}, device_id_type=mesh_id)

    def backward(q):
        return pltpu.make_async_remote_copy(
            src_ref=adjoint_out.at[q], dst_ref=back_ref.at[q], send_sem=send_b.at[q],
            recv_sem=recv_b.at[q], device_id={"seq": earlier}, device_id_type=mesh_id)

    @pl.loop(0, pair_count)
    def _(q):
        @pl.loop(1, head_count)
        def _(i):
            cotangent(i, q).start()

    ends = doc_ends(lengths_ref)
    for k in range(blocks):
        span = slice(k * GROUP, (k + 1) * GROUP)
        at = me * rows + k * GROUP
        here, from_mask[k], to_mask[k] = block_masks(ends, at)
        across = doc_of(at + iota(1), ends)
        inner = ndot(c_ref[span], b_ref[span])
        inner_ref[k] = jnp.where((here == across) & (iota(0) >= iota(1)), inner, 0.0)
        inner_t = ndot(b_ref[span], c_ref[span])
        inner_t_ref[k] = jnp.where((here == across) & (iota(0) <= iota(1)), inner_t, 0.0)
        bt = b_ref[span].astype(F32).T.astype(BF16)
        ct = c_ref[span].astype(F32).T.astype(BF16)
        b_t[k] = jnp.concatenate([bt, bt], axis=1)
        c_t[k] = jnp.concatenate([ct, ct], axis=1)
    own.wait()
    lower = (iota(1) <= iota(0)).astype(F32)

    upper = (iota(0) <= iota(1)).astype(F32)
    lane_head = iota(1) // HEAD_DIM

    def stack(value):
        zero = jnp.zeros_like(value)
        return jnp.concatenate([jnp.where(lane_head == h, value, zero) for h in range(PAIR)], axis=0)

    def runs_of(q):
        runs = []
        for k in range(blocks):
            rates = rates_ref[q, :, k * GROUP : (k + 1) * GROUP]
            line = jnp.dot(rates, upper, precision=EXACT, preferred_element_type=F32)
            runs.append((line,) + pair_columns(running_columns(rates, lower), 0))
        return runs

    def forward_step(q):
        state = jnp.zeros((b_ref.shape[1], LANES), F32)
        decay = jnp.ones((1, LANES), F32)
        runs = runs_of(q)
        kept = []
        for k, (_, _, run) in enumerate(runs):
            total = run[GROUP - 1 : GROUP]
            go = jnp.exp(run - total) * to_mask[k]
            end = jnp.exp(-total) * from_mask[k, GROUP - 1 : GROUP]
            x = x_ref[k * GROUP : (k + 1) * GROUP, lanes_of(q)].astype(F32)
            add = dot(b_t[k], split(go * x, 0))
            state = end * state + add
            decay = decay * end
            kept.append((end, add))

        @pl.when(first)
        def _():
            into_ref[q] = jnp.zeros_like(state)
            state_out[q] = state
            forward(q).start()

        @pl.when(jnp.logical_not(first))
        def _():
            forward(q).wait_recv()

            @pl.when(jnp.logical_not(last))
            def _():
                state_out[q] = decay * into_ref[q] + state
                forward(q).start()

        state = into_ref[q]
        for k, (line, wide, run) in enumerate(runs):
            span = slice(k * GROUP, (k + 1) * GROUP)
            inner = inner_ref[k]
            scores = jnp.concatenate(
                [(jnp.exp(jnp.minimum(line[h : h + 1] - wide[h], 0.0)) * inner).astype(BF16)
                 for h in range(PAIR)], axis=1)
            x = x_ref[span, lanes_of(q)]
            c = c_ref[span]
            come = jnp.exp(-run) * from_mask[k]
            carried = come * dot(jnp.concatenate([c, c], axis=1), split(state, 0))
            y_ref[span, lanes_of(q)] = (
                dot(scores, stack(x)) + carried + skip_ref[q] * x.astype(F32)
            ).astype(BF16)
            end, add = kept[k]
            state = end * state + add

    def backward_step(q):
        @pl.loop(1, head_count)
        def _(i):
            cotangent(i, q).wait_recv()

        adjoint = jnp.zeros((b_ref.shape[1], LANES), F32)
        decay = jnp.ones((1, LANES), F32)
        partial = jnp.zeros((GROUP, LANES), F32)
        runs = runs_of(q)
        kept = [None] * blocks
        for k in reversed(range(blocks)):
            come = jnp.exp(-runs[k][2]) * from_mask[k]
            end = come[GROUP - 1 : GROUP]
            x = x_ref[k * GROUP : (k + 1) * GROUP, lanes_of(q)].astype(F32)
            g = g_ref[k * GROUP : (k + 1) * GROUP, lanes_of(q)].astype(F32)
            partial = partial + x * g
            add = dot(c_t[k], split(come * g, 0))
            adjoint = end * adjoint + add
            decay = decay * end
            kept[k] = (end, add)
        partial_ref[pl.ds(q, 1)] = jnp.sum(partial, axis=0, keepdims=True)

        @pl.when(last)
        def _():
            back_ref[q] = jnp.zeros_like(adjoint)
            adjoint_out[q] = adjoint
            backward(q).start()

        @pl.when(jnp.logical_not(last))
        def _():
            backward(q).wait_recv()

            @pl.when(jnp.logical_not(first))
            def _():
                adjoint_out[q] = decay * back_ref[q] + adjoint
                backward(q).start()

        adjoint = back_ref[q]
        for k in reversed(range(blocks)):
            span = slice(k * GROUP, (k + 1) * GROUP)
            line, wide, run = runs[k]
            inner = inner_t_ref[k]
            scores = jnp.concatenate(
                [(jnp.exp(jnp.minimum(wide[h] - line[h : h + 1], 0.0)) * inner).astype(BF16)
                 for h in range(PAIR)], axis=1)
            g = g_ref[span, lanes_of(q)]
            b = b_ref[span]
            go = jnp.exp(run - run[GROUP - 1 : GROUP]) * to_mask[k]
            carried = go * dot(jnp.concatenate([b, b], axis=1), split(adjoint, 0))
            gx_ref[span, lanes_of(q)] = (
                dot(scores, stack(g)) + carried + skip_ref[q] * g.astype(F32)
            ).astype(BF16)
            end, add = kept[k]
            adjoint = end * adjoint + add

    @pl.loop(0, pair_count + LAG * (count - 1))
    def _(t):
        q = t - LAG * me
        r = t - LAG * (count - 1 - me)

        @pl.when((q >= 0) & (q < pair_count))
        def _():
            forward_step(q)

        @pl.when((r >= 0) & (r < pair_count))
        def _():
            backward_step(r)

    @pl.loop(1, copies)
    def _(i):
        part(i).start()

    gathered_ref[copy_me] = partial_ref[...]

    @pl.loop(0, pair_count)
    def _(q):
        @pl.loop(1, head_count)
        def _(i):
            cotangent(i, q).wait_send()

        @pl.when(jnp.logical_not(last))
        def _():
            forward(q).wait_send()

        @pl.when(jnp.logical_not(first))
        def _():
            backward(q).wait_send()

    @pl.loop(1, copies)
    def _(i):
        part(i).wait()

    total = gathered_ref[0]
    for other in range(1, copies):
        total = total + gathered_ref[other]
    lane = lax.broadcasted_iota(jnp.int32, total.shape, 1) // HEAD_DIM
    sums_ref[...] = jnp.concatenate(
        [jnp.sum(jnp.where(lane == h, total, 0.0), axis=1, keepdims=True) for h in range(PAIR)],
        axis=1) / scale


def shards(x_in, b_in, c_in, rates, skip, doc_lengths, grad_y):
    _, rows, width = x_in.shape
    heads = skip.shape[0]
    state_dim = b_in.shape[2]
    pairs = width // LANES
    blocks = rows // GROUP
    peers = lax.axis_size("head") - 1
    copies = lax.axis_size("dp") * lax.axis_size("seq")
    tokens_all = copies * rows * HEAD_DIM
    gains = jnp.repeat(skip, HEAD_DIM).reshape(pairs, 1, LANES)
    vmem = pl.BlockSpec(memory_space=pltpu.VMEM)
    dma = pltpu.SemaphoreType.DMA
    shape = jax.ShapeDtypeStruct((rows, width), BF16)
    states = pltpu.VMEM((pairs, state_dim, LANES), F32)
    square = pltpu.VMEM((blocks, GROUP, GROUP), F32)
    twice = pltpu.VMEM((blocks, state_dim, 2 * GROUP), BF16)
    y, gx, sums = pl.pallas_call(
        functools.partial(exchange_kernel, math.sqrt(tokens_all)),
        in_specs=[pl.BlockSpec(memory_space=pltpu.SMEM)] + [vmem] * 6,
        out_specs=[vmem] * 3,
        out_shape=[shape, shape, jax.ShapeDtypeStruct((pairs, PAIR), F32)],
        scratch_shapes=[
            pltpu.VMEM((rows, width), BF16), states, states,
            pltpu.VMEM((pairs, LANES), F32), pltpu.VMEM((copies, pairs, LANES), F32),
            states, states, square, square, twice, twice, square, square,
        ] + [dma((pairs,))] * 4 + [dma((peers, pairs))] * 2 + [dma((copies - 1,))] * 2 + [dma],
        compiler_params=pltpu.CompilerParams(collective_id=0, has_side_effects=True),
        name="exchange",
    )(doc_lengths, x_in[0], grad_y[0], b_in[0], c_in[0], rates.reshape(pairs, PAIR, rows), gains)
    return y[None], gx[None], sums.reshape(heads)


def solution(mesh):
    placed = (
        P("dp", "seq", "head"),
        P("dp", "seq", None),
        P("dp", "seq", None),
        P("dp", "head", "seq"),
        P("head"),
        P("dp", None),
        P("dp", ("seq", "head"), None),
    )
    return jax.shard_map(
        shards,
        mesh=mesh,
        in_specs=placed,
        out_specs=(P("dp", "seq", "head"), P("dp", "seq", "head"), P("head")),
        check_vma=False,
    )
```

time: 80.1 us -> 73.9 us (0.923)
  Pallas kernels: 70.3 us -> 64 us
  local copies, waits for them, and re-layouts: 3.6 us -> 8.95 us
  waiting for transfers between devices: 3.2 us -> 0 us
  other arithmetic: 2 us -> 0 us
    pallas_call x2 -> x1, Pallas kernels: 70.3 us -> 64 us  [shards(): pl.pallas_call(functools.partial(exchange_kernel, math.sqrt(tokens_all)),...]
    unnamed x4, local copies, waits for them, and re-layouts: 0.01 us -> 4.63 us
    ppermute x3 -> x0, waiting for transfers between devices: 3.2 us -> none  [total_over(): other = lax.ppermute(value, axis, [(i, i ^ step) for i in range(count)])]
    pallas_call x1 -> x0, other arithmetic: 1.36 us -> none  [shards(): pl.pallas_call(exchange_kernel, in_specs=[lengths_spec] + [vmem] * 5, out...]
    reshape x3 -> x2, local copies, waits for them, and re-layouts: 2.23 us -> 2.8 us  [the longest x1 1.5 us: shards(): rates.reshape(pairs, PAIR, rows)]
  transfers between devices with their start and end apart: 3 -> 0, of which waited for: 2 -> 0; matrix products, arithmetic and copies ran while one was open for 2% -> 0% of each run, Pallas kernels for 23% -> 0%
where the time goes in v3:
time: 73.9 us; the launch traced here: 73.6 us
  Pallas kernels  64 us (87%)
  local copies, waits for them, and re-layouts  8.95 us (12%)
    pallas_call x1, Pallas kernels, shards(): pl.pallas_call(functools.partial(exchange_kernel, math.sqrt(tokens_all)),...  64 us
    unnamed x4, local copies, waits for them, and re-layouts  4.63 us
    broadcast_in_dim x3, local copies, waits for them, and re-layouts, shards(): gains = jnp.repeat(skip, HEAD_DIM).reshape(pairs, 1, LANES)  1.52 us
    reshape x1, local copies, waits for them, and re-layouts, shards(): rates.reshape(pairs, PAIR, rows)  1.5 us

profile of v3, /device:TPU:0, one launch (start us, length us, event | category | flops | bytes accessed | tf_op | source)
XLA Modules:
  0.0 73.6 jit_solution(13451862102044746075)
XLA Ops:
  0.6 0.7 broadcast_in_dim.13
  1.4 0.1 broadcast_in_dim.14
  1.4 0.7 broadcast_in_dim.15.skip_ref
  2.1 1.5 %reshape.19.rates_ref = f32[16,2,512]{2,1,0:T(2,128)} reshape(f32[1,32,512]{2,1,0:T(8,128)} %param.10) | data formatting | bytes 131072 | tf_op jit(solution)/shard_map/reshape | solution.py:366
  3.7 64.0 %exchange.1 = (bf16[512,2048]{1,0:T(8,128)(2,1)}, bf16[512,2048]{1,0:T(8,128)(2,1)}, f32[16,2]{1,0:T(8,128)}) custom-call(s32[1,8]{1,0:T(1,128)} %lengths_ref.1, bf16[512,2048]{1,0:T(8,128)(2,1)} %bitcast.6, bf16[128,8192]{1,0:T(8,128)(2,1)} %bitcast.7, bf16[512,128]{1,0:T(8,128)(2,1)} %bitcast.10, bf16[512,128]{1,0:T(8,128)(2,1)} %bitcast.11, ...), custom_call_target="tpu_custom_call" | custom-call | tf_op jit(solution)/shard_map/exchange/pallas_call | solution.py:354
  67.7 1.3 %reshape.20 = f32[32]{0:T(128)} reshape(f32[16,2]{1,0:T(8,128)} %get-tuple-element.8) | data formatting | bytes 256 | tf_op jit(solution)/shard_map/reshape | solution.py:367
  69.0 0.0 copy-start
  69.0 3.3 %copy.12 = bf16[1,512,2048]{2,1,0:T(8,128)(2,1)} copy(bf16[1,512,2048]{2,1,0:T(8,128)(2,1)} %bitcast.9) | data formatting | bytes 4194304
  72.3 0.0 copy-done
  72.3 1.3 %copy.13 = bf16[1,512,2048]{2,1,0:T(8,128)(2,1)} copy(bf16[1,512,2048]{2,1,0:T(8,128)(2,1)S(1)} %bitcast.8) | data formatting | bytes 4194304
Async XLA Ops:
  69.0 3.3 %copy-start = (bf16[512,2048]{1,0:T(8,128)(2,1)S(1)}, bf16[512,2048]{1,0:T(8,128)(2,1)}, u32[]{:S(2)}) copy-start(bf16[512,2048]{1,0:T(8,128)(2,1)} %get-tuple-element.7) | copy-start | bytes 6291460

commit v4 on v3

--- a/solution.py
+++ b/solution.py
@@ -77,13 +77,14 @@
     return wide, joined
 
 
-LAG = 2
+LAG = 3
 
 
 def exchange_kernel(scale, lengths_ref, x_ref, gy_ref, b_ref, c_ref, rates_ref, skip_ref,
                     y_ref, gx_ref, sums_ref,
                     g_ref, into_ref, back_ref, partial_ref, gathered_ref,
                     state_out, adjoint_out, from_mask, to_mask, b_t, c_t, inner_ref, inner_t_ref,
+                    lines_ref, columns_ref,
                     send_f, recv_f, send_b, recv_b, send_g, recv_g, send_p, recv_p, own_sem):
     rows, width = x_ref.shape
     blocks = rows // GROUP
@@ -179,13 +180,28 @@
         zero = jnp.zeros_like(value)
         return jnp.concatenate([jnp.where(lane_head == h, value, zero) for h in range(PAIR)], axis=0)
 
+    for k in range(blocks):
+        span = slice(k * GROUP, (k + 1) * GROUP)
+        rates = rates_ref[:, span]
+        lines = jnp.dot(rates, upper, precision=EXACT, preferred_element_type=F32)
+        columns = running_columns(rates, lower)
+        for pair in range(pair_count):
+            heads = slice(pair * PAIR, (pair + 1) * PAIR)
+            lines_ref[pair, :, span] = lines[heads]
+            columns_ref[pair, span] = columns[:, heads]
+
     def runs_of(q):
         runs = []
         for k in range(blocks):
-            rates = rates_ref[q, :, k * GROUP : (k + 1) * GROUP]
-            line = jnp.dot(rates, upper, precision=EXACT, preferred_element_type=F32)
-            runs.append((line,) + pair_columns(running_columns(rates, lower), 0))
+            span = slice(k * GROUP, (k + 1) * GROUP)
+            runs.append((lines_ref[q, :, span],) + pair_columns(columns_ref[q, span], 0))
         return runs
+
+    def gain_of(q):
+        gain = jnp.full((GROUP, LANES), skip_ref[q * PAIR], F32)
+        for h in range(1, PAIR):
+            gain = jnp.where(lane_head == h, skip_ref[q * PAIR + h], gain)
+        return gain
 
     def forward_step(q):
         state = jnp.zeros((b_ref.shape[1], LANES), F32)
@@ -218,6 +234,7 @@
                 forward(q).start()
 
         state = into_ref[q]
+        gain = gain_of(q)
         for k, (line, wide, run) in enumerate(runs):
             span = slice(k * GROUP, (k + 1) * GROUP)
             inner = inner_ref[k]
@@ -229,7 +246,7 @@
             come = jnp.exp(-run) * from_mask[k]
             carried = come * dot(jnp.concatenate([c, c], axis=1), split(state, 0))
             y_ref[span, lanes_of(q)] = (
-                dot(scores, stack(x)) + carried + skip_ref[q] * x.astype(F32)
+                dot(scores, stack(x)) + carried + gain * x.astype(F32)
             ).astype(BF16)
             end, add = kept[k]
             state = end * state + add
@@ -272,6 +289,7 @@
                 backward(q).start()
 
         adjoint = back_ref[q]
+        gain = gain_of(q)
         for k in reversed(range(blocks)):
             span = slice(k * GROUP, (k + 1) * GROUP)
             line, wide, run = runs[k]
@@ -284,7 +302,7 @@
             go = jnp.exp(run - run[GROUP - 1 : GROUP]) * to_mask[k]
             carried = go * dot(jnp.concatenate([b, b], axis=1), split(adjoint, 0))
             gx_ref[span, lanes_of(q)] = (
-                dot(scores, stack(g)) + carried + skip_ref[q] * g.astype(F32)
+                dot(scores, stack(g)) + carried + gain * g.astype(F32)
             ).astype(BF16)
             end, add = kept[k]
             adjoint = end * adjoint + add
@@ -344,7 +362,7 @@
     peers = lax.axis_size("head") - 1
     copies = lax.axis_size("dp") * lax.axis_size("seq")
     tokens_all = copies * rows * HEAD_DIM
-    gains = jnp.repeat(skip, HEAD_DIM).reshape(pairs, 1, LANES)
+    smem = pl.BlockSpec(memory_space=pltpu.SMEM)
     vmem = pl.BlockSpec(memory_space=pltpu.VMEM)
     dma = pltpu.SemaphoreType.DMA
     shape = jax.ShapeDtypeStruct((rows, width), BF16)
@@ -353,17 +371,18 @@
     twice = pltpu.VMEM((blocks, state_dim, 2 * GROUP), BF16)
     y, gx, sums = pl.pallas_call(
         functools.partial(exchange_kernel, math.sqrt(tokens_all)),
-        in_specs=[pl.BlockSpec(memory_space=pltpu.SMEM)] + [vmem] * 6,
+        in_specs=[smem] + [vmem] * 5 + [smem],
         out_specs=[vmem] * 3,
         out_shape=[shape, shape, jax.ShapeDtypeStruct((pairs, PAIR), F32)],
         scratch_shapes=[
             pltpu.VMEM((rows, width), BF16), states, states,
             pltpu.VMEM((pairs, LANES), F32), pltpu.VMEM((copies, pairs, LANES), F32),
             states, states, square, square, twice, twice, square, square,
+            pltpu.VMEM((pairs, PAIR, rows), F32), pltpu.VMEM((pairs, rows, PAIR), F32),
         ] + [dma((pairs,))] * 4 + [dma((peers, pairs))] * 2 + [dma((copies - 1,))] * 2 + [dma],
         compiler_params=pltpu.CompilerParams(collective_id=0, has_side_effects=True),
         name="exchange",
-    )(doc_lengths, x_in[0], grad_y[0], b_in[0], c_in[0], rates.reshape(pairs, PAIR, rows), gains)
+    )(doc_lengths, x_in[0], grad_y[0], b_in[0], c_in[0], rates[0], skip)
     return y[None], gx[None], sums.reshape(heads)
 
 

time: 73.9 us -> 60.5 us (0.82)
  Pallas kernels: 64 us -> 53.7 us
  local copies, waits for them, and re-layouts: 8.95 us -> 5.93 us
    pallas_call x1, Pallas kernels: 64 us -> 53.7 us  [shards(): pl.pallas_call(functools.partial(exchange_kernel, math.sqrt(tokens_all)),...]
    broadcast_in_dim x3 -> x0, local copies, waits for them, and re-layouts: 1.52 us -> none  [shards(): gains = jnp.repeat(skip, HEAD_DIM).reshape(pairs, 1, LANES)]
    reshape x1 -> x0, local copies, waits for them, and re-layouts: 1.5 us -> none  [shards(): rates.reshape(pairs, PAIR, rows)]
where the time goes in v4:
time: 60.5 us; the launch traced here: 60.3 us
  Pallas kernels  53.7 us (89%)
  local copies, waits for them, and re-layouts  5.93 us (10%)
  between operations  0.64 us (1%)
    pallas_call x1, Pallas kernels, shards(): pl.pallas_call(functools.partial(exchange_kernel, math.sqrt(tokens_all)),...  53.7 us
    unnamed x4, local copies, waits for them, and re-layouts  4.63 us
    reshape x1, local copies, waits for them, and re-layouts, shards(): return (y[None], gx[None], sums.reshape(heads))  1.3 us

profile of v4, /device:TPU:0, one launch (start us, length us, event | category | flops | bytes accessed | tf_op | source)
XLA Modules:
  0.0 60.3 jit_solution(13313624637715536195)
XLA Ops:
  0.6 53.7 %exchange.1 = (bf16[512,2048]{1,0:T(8,128)(2,1)}, bf16[512,2048]{1,0:T(8,128)(2,1)}, f32[16,2]{1,0:T(8,128)}) custom-call(s32[1,8]{1,0:T(1,128)} %lengths_ref.1, bf16[512,2048]{1,0:T(8,128)(2,1)} %bitcast.7, bf16[128,8192]{1,0:T(8,128)(2,1)} %bitcast.8, bf16[512,128]{1,0:T(8,128)(2,1)} %bitcast.11, bf16[512,128]{1,0:T(8,128)(2,1)} %bitcast.12, ...), custom_call_target="tpu_custom_call" | custom-call | tf_op jit(solution)/shard_map/exchange/pallas_call | solution.py:372
  54.4 1.3 %reshape.9 = f32[32]{0:T(128)} reshape(f32[16,2]{1,0:T(8,128)} %get-tuple-element.8) | data formatting | bytes 256 | tf_op jit(solution)/shard_map/reshape | solution.py:386
  55.7 0.0 copy-start
  55.7 3.3 %copy.12 = bf16[1,512,2048]{2,1,0:T(8,128)(2,1)} copy(bf16[1,512,2048]{2,1,0:T(8,128)(2,1)} %bitcast.10) | data formatting | bytes 4194304
  59.0 0.0 copy-done
  59.0 1.3 %copy.13 = bf16[1,512,2048]{2,1,0:T(8,128)(2,1)} copy(bf16[1,512,2048]{2,1,0:T(8,128)(2,1)S(1)} %bitcast.9) | data formatting | bytes 4194304
Async XLA Ops:
  55.7 3.3 %copy-start = (bf16[512,2048]{1,0:T(8,128)(2,1)S(1)}, bf16[512,2048]{1,0:T(8,128)(2,1)}, u32[]{:S(2)}) copy-start(bf16[512,2048]{1,0:T(8,128)(2,1)} %get-tuple-element.7) | copy-start | bytes 6291460
